TPU v7x, 512 devices: a whole 4x8x8 slice. The times are simulated.
512 devices in a mesh: dom: 32 (over z, x), band: 16 (over y, core).
Axes of the slice: x: 4, y: 8, z: 8, core: 2. Of those that a mesh axis runs over, the one named last changes fastest.
Arguments:
- waves: float32 [256, 131072], P('band', 'dom'), may hold values from -6 to 6
- potential: float32 [131072], P('dom'), may hold values from 0 to 4
- atom_points: int32 [128, 256], P('dom'), may hold values from 0 to 4095
- projectors: float32 [128, 8, 256], P('dom'), may hold values from -0.75 to 0.75
- coupling: float32 [128, 8, 8], P('dom'), may hold values from -1 to 1
Outputs:
- ortho: float32 [256, 131072], P('band', 'dom')
Inputs may be any that keep to these rules, and one draw needn't show every extreme that they name: `atom_points`: an index of a point within the atom's own subdomain, repeats allowed.
All inputs are finite; a program needn't handle non-finite values.
Results may differ from a plain program's by a relative error of at most 0.0003.
Values sent between devices are 32-bit elements; how exact they have to be, the bound alone decides.
A program may use at most 64 MiB of HBM per device.

v0:
```python
import jax
import jax.numpy as jnp
from jax import lax
from jax.sharding import PartitionSpec as P

CUBE = 16


high = lax.Precision.HIGHEST


def passed_along(value, axis, by):
    size = lax.axis_size(axis)
    pairs = [(i, i + by) for i in range(size) if 0 <= i + by < size]
    return lax.ppermute(value, axis, pairs)


def shifted(face, offset):
    return passed_along(face, "dom", offset)


def laplace(grid, coords, counts, strides):
    total = -7.5 * grid
    for dim in range(3):
        axis = dim + 1
        lower_face = lax.slice_in_dim(grid, 0, 2, axis=axis)
        upper_face = lax.slice_in_dim(grid, CUBE - 2, CUBE, axis=axis)
        above = shifted(lower_face, -strides[dim]) * (coords[dim] < counts[dim] - 1).astype(
            jnp.float32
        )
        below = shifted(upper_face, strides[dim]) * (coords[dim] > 0).astype(jnp.float32)
        padded = jnp.concatenate([below, grid, above], axis=axis)

        def part(offset):
            return lax.slice_in_dim(padded, offset, offset + CUBE, axis=axis)

        total = total + 4.0 / 3.0 * (part(1) + part(3)) - 1.0 / 12.0 * (part(0) + part(4))
    return total


def nonlocal_one(values, points, proj, coup):
    picked = values[:, points]
    coef = jnp.einsum("aks,bas->bak", proj, picked, precision=high)
    mixed = jnp.einsum("akj,baj->bak", coup, coef, precision=high)
    spread = jnp.einsum("aks,bak->bas", proj, mixed, precision=high)
    return jnp.zeros_like(values).at[:, points.reshape(-1)].add(spread.reshape(values.shape[0], -1))


def local(waves, potential, atom_points, projectors, coupling):
    groups, local_points = waves.shape
    dom_count = lax.axis_size("dom")
    depth_z = 2
    depth_y = min(4, dom_count // 2)
    depth_x = dom_count // (depth_z * depth_y)
    where = lax.axis_index("dom")
    coords = (where // (depth_y * depth_z), where // depth_z % depth_y, where % depth_z)
    counts = (depth_x, depth_y, depth_z)
    strides = (depth_y * depth_z, depth_z, 1)

    def apply_h(values):
        grid = values.reshape(groups, CUBE, CUBE, CUBE)
        kinetic = laplace(grid, coords, counts, strides).reshape(groups, local_points)
        extra = nonlocal_one(values, atom_points, projectors, coupling)
        return -0.5 * kinetic + potential[None, :] * values + extra

    first = (apply_h(waves) - 6.0 * waves) / 4.0
    filtered = 2.0 * (apply_h(first) - 6.0 * first) / 4.0 - waves
    pieces = lax.all_to_all(filtered, "band", split_axis=1, concat_axis=0, tiled=True)
    scale = 1.0 / (dom_count * local_points)
    partial_value = (
        jnp.dot(pieces, pieces.T, precision=high, preferred_element_type=jnp.float32) * scale
    )
    gram = lax.psum(partial_value, ("dom", "band"))
    lower = jnp.linalg.cholesky(gram)
    rotated = jax.scipy.linalg.solve_triangular(lower, pieces, lower=True)
    return lax.all_to_all(rotated, "band", split_axis=0, concat_axis=1, tiled=True)


def solution(mesh):
    placed = (
        P("band", "dom"),
        P("dom"),
        P("dom", None),
        P("dom", None, None),
        P("dom", None, None),
    )
    return jax.shard_map(
        local, mesh=mesh, in_specs=placed, out_specs=P("band", "dom"), check_vma=False
    )
```

profile of v0, /device:TPU:1, one launch (start us, length us, event | category | flops | bytes accessed | tf_op | source)
XLA Modules:
  0.0 548.6 jit_solution(12536738940076583858)
XLA Ops:
  6.5 1.7 reshape.78
  8.2 2.7 fusion.58
  10.9 3.1 copy.102
  14.0 4.6 collective-permute-start.4
  18.7 3.9 copy.105
  22.6 1.4 collective-permute-start.5
  25.1 5.5 %collective-permute-start.2 = (f32[16,16,2,16]{3,2,1,0:T(2,128)}, f32[16,16,2,16]{3,2,1,0:T(2,128)}, u32[]{:S(2)}, u32[]{:S(2)}) collective-permute-start(f32[16,16,2,16]{3,2,1,0:T(2,128)} %get-tuple-element.31), channel_id=1, source_target_pairs={{0,32},{16,48},{32,64},{48,80},{64,96},{80,112},{96,128},{112,144}... | collective-permute-start | bytes 98312 | tf_op jit(solution)/shard_map/ppermute | solution.py:15
  30.6 1.4 collective-permute-start.3
  32.9 9.7 %collective-permute-start = (f32[16,2,16,16]{3,2,1,0:T(8,128)}, f32[16,2,16,16]{3,2,1,0:T(8,128)}, u32[]{:S(2)}, u32[]{:S(2)}) collective-permute-start(f32[16,2,16,16]{3,2,1,0:T(8,128)} %get-tuple-element.33), channel_id=1, source_target_pairs={{0,128},{16,144},{32,160},{48,176},{64,192},{80,208},{96,224},{112... | collective-permute-start | bytes 98312 | tf_op jit(solution)/shard_map/ppermute | solution.py:15
  42.6 2.0 copy.108
  44.6 4.4 gather_fusion
  51.5 1.3 collective-permute-start.1
  54.8 1.7 broadcast_multiply_fusion.1
  57.4 2.9 copy.104
  60.3 3.8 copy.107
  64.2 7.2 %collective-permute-done.1 = f32[16,2,16,16]{3,2,1,0:T(8,128)} collective-permute-done((f32[16,2,16,16]{3,2,1,0:T(8,128)}, f32[16,2,16,16]{3,2,1,0:T(8,128)}, u32[]{:S(2)}, u32[]{:S(2)}) %collective-permute-start.1) | collective-permute-done | bytes 32800 | tf_op jit(solution)/shard_map/ppermute | solution.py:15
  72.3 8.1 %fusion.20 = f32[16,16,16,16]{3,2,1,0:T(8,128)} fusion(f32[16,16,16,16]{3,2,1,0:T(8,128)S(1)} %reshape.78, f32[16,2,16,16]{3,2,1,0:T(8,128)S(1)} %broadcast_multiply_fusion.10, f32[16,2,16,16]{3,2,1,0:T(8,128)S(1)} %broadcast_multiply_fusion.12, f32[16,16,2,16]{3,2,1,0:T(2,128)S(1)} %bitcast.110, f32[16,16,2,16]{3,2,1,0:T(2,128)S(1)} %bitcast.108, ...), kind=kLoop, calls=%fused_computation.42 | loop fusion | flops 2097152 | bytes 720896 | tf_op jit(solution)/shard_map/mul | solution.py:64
  80.5 3.1 mul.170
  84.3 7.4 %scatter_fusion = f32[16,4096]{0,1:T(8,128)S(1)} fusion(f32[16,4096]{0,1:T(8,128)S(1)} %copy.111, s32[1024]{0:T(1024)S(1)} %bitcast.121, f32[1024,16]{1,0:T(8,128)} %copy.112), kind=kCustom, calls=%fused_computation.2 | custom fusion | flops 16384 | bytes 200704 | tf_op jit(solution)/shard_map/scatter-add | solution.py:46
  93.0 2.8 fusion.55
  97.6 2.0 copy.120
  99.6 3.1 copy.114
  102.7 2.0 collective-permute-start.10
  104.7 3.9 copy.117
  108.6 1.3 collective-permute-start.11
  109.9 4.0 collective-permute-start.8
  113.9 1.3 collective-permute-start.9
  115.2 13.4 %collective-permute-start.6 = (f32[16,2,16,16]{3,2,1,0:T(8,128)}, f32[16,2,16,16]{3,2,1,0:T(8,128)}, u32[]{:S(2)}, u32[]{:S(2)}) collective-permute-start(f32[16,2,16,16]{3,2,1,0:T(8,128)} %get-tuple-element.27), channel_id=1, source_target_pairs={{0,128},{16,144},{32,160},{48,176},{64,192},{80,208},{96,224},{112... | collective-permute-start | bytes 98312 | tf_op jit(solution)/shard_map/ppermute | solution.py:15
  128.6 4.4 gather_fusion.1
  134.8 1.3 collective-permute-start.7
  139.0 1.7 broadcast_multiply_fusion
  140.7 1.7 broadcast_multiply_fusion.11
  142.4 2.9 copy.116
  145.3 3.9 copy.119
  150.2 8.1 %fusion.9 = f32[16,16,16,16]{3,2,1,0:T(8,128)} fusion(f32[16,16,16,16]{3,2,1,0:T(8,128)S(1)} %reshape.81, f32[16,2,16,16]{3,2,1,0:T(8,128)S(1)} %broadcast_multiply_fusion.9, f32[16,2,16,16]{3,2,1,0:T(8,128)S(1)} %copy-done.2, f32[16,16,2,16]{3,2,1,0:T(2,128)S(1)} %bitcast.109, f32[16,16,2,16]{3,2,1,0:T(2,128)S(1)} %bitcast.107, ...), kind=kLoop, calls=%fused_computation.31 | loop fusion | flops 2097152 | bytes 720896 | tf_op jit(solution)/shard_map/mul | solution.py:64
  158.3 3.1 mul.188
  162.1 7.2 %scatter_fusion.1 = f32[16,4096]{0,1:T(8,128)S(1)} fusion(f32[16,4096]{0,1:T(8,128)S(1)} %copy.123, s32[1024]{0:T(1024)S(1)} %bitcast.122, f32[1024,16]{1,0:T(8,128)} %copy.124), kind=kCustom, calls=%fused_computation.3 | custom fusion | flops 16384 | bytes 200704 | tf_op jit(solution)/shard_map/scatter-add | solution.py:46
  170.6 9.0 %all-to-all-start = ((f32[16,16,256]{2,0,1:T(8,128)}), f32[16,16,256]{2,0,1:T(8,128)S(1)}, u32[]{:S(2)}, u32[]{:S(2)}) async-start(f32[16,16,256]{2,0,1:T(8,128)} %bitcast.90), calls=%async_computation | async-start | bytes 524288 | tf_op jit(solution)/shard_map/all_to_all | solution.py:68
  179.9 11.3 %all-to-all-done = f32[16,16,256]{2,0,1:T(8,128)S(1)} async-done(((f32[16,16,256]{2,0,1:T(8,128)}), f32[16,16,256]{2,0,1:T(8,128)S(1)}, u32[]{:S(2)}, u32[]{:S(2)}) %all-to-all-start) | async-done | bytes 262176 | tf_op jit(solution)/shard_map/all_to_all | solution.py:68
  192.4 267.4 %all-reduce.3.cloned.1.call-done = f32[256,256]{0,1:T(8,128)} async-done(((f32[256,256]{0,1:T(8,128)}), f32[256,256]{0,1:T(8,128)}) %all-reduce.3.cloned.1.call-update) | async-done | bytes 262160 | tf_op jit(solution)/shard_map/psum | solution.py:73
  461.9 11.7 %cholesky.50 = f32[128,128]{1,0:T(8,128)S(1)} custom-call(f32[128,128]{1,0:T(8,128)S(1)} %cholesky.118), custom_call_target="Cholesky" | custom-call | tf_op jit(solution)/shard_map/jit(cholesky)/cholesky | solution.py:74
  473.7 9.8 %custom-call.15 = f32[1,128,128]{1,2,0:T(8,128)S(1)} custom-call(f32[1,128,128]{2,1,0:T(8,128)S(1)} %get-tuple-element.40), custom_call_target="InvertDiagBlocksLowerTriangular" | custom-call | tf_op jit(solution)/shard_map/jit(cholesky)/cholesky | solution.py:74
  484.0 11.7 %cholesky.105 = f32[128,128]{1,0:T(8,128)S(1)} custom-call(f32[128,128]{1,0:T(8,128)S(1)} %convolution_subtract_fusion.1), custom_call_target="Cholesky" | custom-call | tf_op jit(solution)/shard_map/jit(cholesky)/cholesky | solution.py:74
  497.9 4.3 while.1
  498.7 1.4 bitcast_dynamic-update-slice_fusion.2
  500.8 1.4 bitcast_dynamic-update-slice_fusion.2
  502.2 19.7 %custom-call.16 = f32[2,128,128]{1,2,0:T(8,128)S(1)} custom-call(f32[2,128,128]{2,1,0:T(8,128)S(1)} %get-tuple-element.12), custom_call_target="InvertDiagBlocksLowerTriangular" | custom-call | tf_op jit(solution)/shard_map/jit(_solve_triangular)/triangular_solve | solution.py:75
  522.9 17.7 %all_to_all.38 = f32[16,16,256]{2,1,0:T(8,128)S(1)} all-to-all(f32[16,16,256]{2,1,0:T(8,128)S(1)} %bitcast.111), channel_id=1, replica_groups=mesh['dom'=32,'band'=16] {'band'}, dimensions={0} | all-to-all | bytes 524288 | tf_op jit(solution)/shard_map/all_to_all | solution.py:76
  (98 shorter events, 27.5 us)
Async XLA Ops:
  6.5 43.2 %copy-start = (f32[4,8,256]{2,1,0:T(8,128)S(1)}, f32[4,8,256]{2,1,0:T(8,128)}, u32[]{:S(2)}) copy-start(f32[4,8,256]{2,1,0:T(8,128)} %param.8) | copy-start | bytes 98308
  14.0 39.8 %collective-permute-start.4 = (f32[16,16,16,2]{2,1,3,0:T(8,128)S(1)}, f32[16,16,16,2]{2,1,3,0:T(8,128)}, u32[]{:S(2)}, u32[]{:S(2)}) collective-permute-start(f32[16,16,16,2]{2,1,3,0:T(8,128)S(1)} %copy.102), channel_id=1, source_target_pairs={{0,16},{16,32},{32,48},{48,64},{64,80},{80,96},{96,112},{112,128},... | collective-permute-start | bytes 98312 | tf_op jit(solution)/shard_map/ppermute | solution.py:15
  18.7 23.9 %copy-start.1 = (f32[16,4096]{1,0:T(8,128)S(1)}, f32[16,4096]{1,0:T(8,128)}, u32[]{:S(2)}) copy-start(f32[16,4096]{1,0:T(8,128)} %param.5) | copy-start | bytes 786436
  22.6 22.0 %copy-start.9 = (s32[4,256]{1,0:T(4,128)S(1)}, s32[4,256]{1,0:T(4,128)}, u32[]{:S(2)}) copy-start(s32[4,256]{1,0:T(4,128)} %param.7) | copy-start | bytes 12292
  22.6 32.2 %collective-permute-start.5 = (f32[16,16,16,2]{2,1,3,0:T(8,128)}, f32[16,16,16,2]{2,1,3,0:T(8,128)}, u32[]{:S(2)}, u32[]{:S(2)}) collective-permute-start(f32[16,16,16,2]{2,1,3,0:T(8,128)} %copy.105), channel_id=1, source_target_pairs={{16,0},{32,16},{48,32},{64,48},{80,64},{96,80},{112,96},{128,112},... | collective-permute-start | bytes 98312 | tf_op jit(solution)/shard_map/ppermute | solution.py:15
  25.1 26.4 %collective-permute-start.2 = (f32[16,16,2,16]{3,2,1,0:T(2,128)}, f32[16,16,2,16]{3,2,1,0:T(2,128)}, u32[]{:S(2)}, u32[]{:S(2)}) collective-permute-start(f32[16,16,2,16]{3,2,1,0:T(2,128)} %get-tuple-element.31), channel_id=1, source_target_pairs={{0,32},{16,48},{32,64},{48,80},{64,96},{80,112},{96,128},{112,144}... | collective-permute-start | bytes 98312 | tf_op jit(solution)/shard_map/ppermute | solution.py:15
  30.6 19.1 %copy-start.4 = (f32[4096]{0:T(1024)S(1)}, f32[4096]{0:T(1024)}, u32[]{:S(2)}) copy-start(f32[4096]{0:T(1024)} %param.6) | copy-start | bytes 49156
  30.6 23.1 %collective-permute-start.3 = (f32[16,16,2,16]{3,2,1,0:T(2,128)}, f32[16,16,2,16]{3,2,1,0:T(2,128)S(1)}, u32[]{:S(2)}, u32[]{:S(2)}) collective-permute-start(f32[16,16,2,16]{3,2,1,0:T(2,128)} %get-tuple-element.32), channel_id=1, source_target_pairs={{32,0},{48,16},{64,32},{80,48},{96,64},{112,80},{128,96},{144,112}... | collective-permute-start | bytes 98312 | tf_op jit(solution)/shard_map/ppermute | solution.py:15
  32.9 17.1 %copy-start.3 = (f32[4,8,8]{2,1,0:T(8,128)S(1)}, f32[4,8,8]{2,1,0:T(8,128)}, u32[]{:S(2)}) copy-start(f32[4,8,8]{2,1,0:T(8,128)} %param.9) | copy-start | bytes 3076
  32.9 23.6 %collective-permute-start = (f32[16,2,16,16]{3,2,1,0:T(8,128)}, f32[16,2,16,16]{3,2,1,0:T(8,128)}, u32[]{:S(2)}, u32[]{:S(2)}) collective-permute-start(f32[16,2,16,16]{3,2,1,0:T(8,128)} %get-tuple-element.33), channel_id=1, source_target_pairs={{0,128},{16,144},{32,160},{48,176},{64,192},{80,208},{96,224},{112... | collective-permute-start | bytes 98312 | tf_op jit(solution)/shard_map/ppermute | solution.py:15
  44.6 4.6 copy-start.7
  51.5 19.9 %collective-permute-start.1 = (f32[16,2,16,16]{3,2,1,0:T(8,128)}, f32[16,2,16,16]{3,2,1,0:T(8,128)}, u32[]{:S(2)}, u32[]{:S(2)}) collective-permute-start(f32[16,2,16,16]{3,2,1,0:T(8,128)} %get-tuple-element.34), channel_id=1, source_target_pairs={{128,0},{144,16},{160,32},{176,48},{192,64},{208,80},{224,96},{240... | collective-permute-start | bytes 98312 | tf_op jit(solution)/shard_map/ppermute | solution.py:15
  83.6 0.7 copy-start.5
  99.6 29.0 %copy-start.8 = (s32[1024]{0:T(1024)S(1)}, s32[1024]{0:T(1024)}, u32[]{:S(2)}) copy-start(s32[1024]{0:T(1024)} %copy-done.7) | copy-start | bytes 12292
  102.7 35.3 %collective-permute-start.10 = (f32[16,16,16,2]{2,1,3,0:T(8,128)S(1)}, f32[16,16,16,2]{2,1,3,0:T(8,128)}, u32[]{:S(2)}, u32[]{:S(2)}) collective-permute-start(f32[16,16,16,2]{2,1,3,0:T(8,128)S(1)} %copy.114), channel_id=1, source_target_pairs={{0,16},{16,32},{32,48},{48,64},{64,80},{80,96},{96,112},{112,128},... | collective-permute-start | bytes 98312 | tf_op jit(solution)/shard_map/ppermute | solution.py:15
  108.6 30.4 %collective-permute-start.11 = (f32[16,16,16,2]{2,1,3,0:T(8,128)}, f32[16,16,16,2]{2,1,3,0:T(8,128)}, u32[]{:S(2)}, u32[]{:S(2)}) collective-permute-start(f32[16,16,16,2]{2,1,3,0:T(8,128)} %copy.117), channel_id=1, source_target_pairs={{16,0},{32,16},{48,32},{64,48},{80,64},{96,80},{112,96},{128,112},... | collective-permute-start | bytes 98312 | tf_op jit(solution)/shard_map/ppermute | solution.py:15
  109.9 24.9 %collective-permute-start.8 = (f32[16,16,2,16]{3,2,1,0:T(2,128)}, f32[16,16,2,16]{3,2,1,0:T(2,128)}, u32[]{:S(2)}, u32[]{:S(2)}) collective-permute-start(f32[16,16,2,16]{3,2,1,0:T(2,128)} %get-tuple-element.25), channel_id=1, source_target_pairs={{0,32},{16,48},{32,64},{48,80},{64,96},{80,112},{96,128},{112,144}... | collective-permute-start | bytes 98312 | tf_op jit(solution)/shard_map/ppermute | solution.py:15
  113.9 23.1 %collective-permute-start.9 = (f32[16,16,2,16]{3,2,1,0:T(2,128)}, f32[16,16,2,16]{3,2,1,0:T(2,128)}, u32[]{:S(2)}, u32[]{:S(2)}) collective-permute-start(f32[16,16,2,16]{3,2,1,0:T(2,128)} %get-tuple-element.26), channel_id=1, source_target_pairs={{32,0},{48,16},{64,32},{80,48},{96,64},{112,80},{128,96},{144,112}... | collective-permute-start | bytes 98312 | tf_op jit(solution)/shard_map/ppermute | solution.py:15
  115.2 25.5 %collective-permute-start.6 = (f32[16,2,16,16]{3,2,1,0:T(8,128)}, f32[16,2,16,16]{3,2,1,0:T(8,128)}, u32[]{:S(2)}, u32[]{:S(2)}) collective-permute-start(f32[16,2,16,16]{3,2,1,0:T(8,128)} %get-tuple-element.27), channel_id=1, source_target_pairs={{0,128},{16,144},{32,160},{48,176},{64,192},{80,208},{96,224},{112... | collective-permute-start | bytes 98312 | tf_op jit(solution)/shard_map/ppermute | solution.py:15
  134.8 14.4 %collective-permute-start.7 = (f32[16,2,16,16]{3,2,1,0:T(8,128)}, f32[16,2,16,16]{3,2,1,0:T(8,128)}, u32[]{:S(2)}, u32[]{:S(2)}) collective-permute-start(f32[16,2,16,16]{3,2,1,0:T(8,128)} %get-tuple-element.28), channel_id=1, source_target_pairs={{128,0},{144,16},{160,32},{176,48},{192,64},{208,80},{224,96},{240... | collective-permute-start | bytes 98312 | tf_op jit(solution)/shard_map/ppermute | solution.py:15
  145.3 4.9 copy-start.2
  161.4 0.7 copy-start.6
  170.6 20.6 %all-to-all-start = ((f32[16,16,256]{2,0,1:T(8,128)}), f32[16,16,256]{2,0,1:T(8,128)S(1)}, u32[]{:S(2)}, u32[]{:S(2)}) async-start(f32[16,16,256]{2,0,1:T(8,128)} %bitcast.90), calls=%async_computation | async-start | bytes 524288 | tf_op jit(solution)/shard_map/all_to_all | solution.py:68
  179.7 280.2 %all-reduce.3.cloned.1.call-start = ((), (), s32[]{:S(2)}) async-start(), calls=%async_computation.2 | async-start | bytes 524288 | tf_op jit(solution)/shard_map/psum | solution.py:73
Sparse Core Ops, SparseCore 0:
  192.5 267.2 all-reduce.2
where the time goes:
time: 558 us; the launch traced here: 549 us
  waiting for transfers between devices  286 us (51%)
  other arithmetic  99.1 us (18%)
  local copies, waits for them, and re-layouts  69.6 us (12%)
  starting transfers between devices  56.5 us (10%)
  blocking collectives  17.7 us (3%)
  between operations  15.7 us (3%)
    psum x1, waiting for transfers between devices, local(): gram = lax.psum(partial_value, ('dom', 'band'))  267 us
    ppermute x12, starting transfers between devices, passed_along(): return lax.ppermute(value, axis, pairs)  47.3 us
    another operation x6, other arithmetic, local(): lower = jnp.linalg.cholesky(gram)  34 us
    another operation x4, other arithmetic, local(): rotated = jax.scipy.linalg.solve_triangular(lower, pieces, lower=True)  19.7 us
    all_to_all x1, blocking collectives, local(): lax.all_to_all(rotated, 'band', split_axis=0, concat_axis=1, tiled=True)  17.7 us
    mul x3, other arithmetic, apply_h(): return -0.5 * kinetic + potential[None, :] * values + extra  16.2 us
    slice x8, local copies, waits for them, and re-layouts, laplace(): upper_face = lax.slice_in_dim(grid, CUBE - 2, CUBE, axis=axis)  15.5 us
    scatter-add x2, other arithmetic, nonlocal_one(): jnp.zeros_like(values).at[:, points.reshape(-1)]  14.5 us
  transfers between devices with their start and end apart: 14, of which 3 were waited for; matrix products, arithmetic and copies ran while one was open for 9% of the time, Pallas kernels for 0%

commit v1 on v0

v1 whole, which is shorter than its diff:
```python
import jax
import jax.numpy as jnp
from jax import lax
from jax.experimental import pallas as pl
from jax.experimental.pallas import tpu as pltpu
from jax.sharding import PartitionSpec as P

F32, BF16 = jnp.float32, jnp.bfloat16
MESH = pl.DeviceIdType.MESH
CUBE = 16
BAND_LOC = 16
PLANE = CUBE * CUBE
POINTS = 131072
NBAND, NZ, NX = 16, 8, 4
ROWS = 17
BLOCK = 32


def iota(shape, dim):
    return lax.broadcasted_iota(jnp.int32, shape, dim)


def split(x):
    big = x.astype(BF16)
    return big, (x - big.astype(F32)).astype(BF16)


def dot(a, b, ca=1, cb=0):
    return lax.dot_general(a, b, (((ca,), (cb,)), ((), ())), preferred_element_type=F32)


def dot3(a, b, ca=1, cb=0):
    ah, al = split(a)
    bh, bl = split(b)
    return dot(ah, bh, ca, cb) + (dot(ah, bl, ca, cb) + dot(al, bh, ca, cb))


def bias(delta):
    step = jnp.abs(delta)
    return jnp.where(step == 1, -16.0, jnp.where(step == 2, 1.0, 0.0))


def kernel(
    waves, pot, pts, proj, coup, out,
    vx0, vx1, pterm, facesend, facerecv, pick, stencil, bhl, ecat, fs, work,
    ptv, projv, coupv, potv, part, rs_buf, z_buf, x_buf, g_buf,
    in_sem, h_send, h_recv, a_send, a_recv, r_send, r_recv, z_send, z_recv, x_send, x_recv,
    g_send, g_recv, o_send, o_recv, o_own,
):
    dom, band = lax.axis_index("dom"), lax.axis_index("band")
    pz, px = dom // NX, lax.rem(dom, NX)
    iz = lax.rem(dom, 2)
    iy = lax.rem(dom // 2, 4)
    ix = dom // 8
    middle = jnp.logical_or(iy == 1, iy == 2)

    copies = [
        pltpu.make_async_copy(
            waves.at[:, pl.ds(PLANE * i, PLANE)], vx0.at[pl.ds(32 + 16 * i, 16), :], in_sem.at[i]
        )
        for i in range(CUBE)
    ]
    small = [
        pltpu.make_async_copy(src, dst, in_sem.at[16 + i])
        for i, (src, dst) in enumerate(((pts, ptv), (proj, projv), (coup, coupv), (pot, potv)))
    ]
    for copy in copies + small:
        copy.start()

    facerecv[...] = jnp.zeros_like(facerecv)
    for ref in (vx0, vx1):
        ref[0:32, :] = jnp.zeros((32, PLANE), F32)
        ref[288:320, :] = jnp.zeros((32, PLANE), F32)

    barrier = pltpu.get_barrier_semaphore()

    def greet(where):
        pl.semaphore_signal(barrier, inc=1, device_id=where, device_id_type=MESH)

    @pl.loop(1, NBAND)
    def _(k):
        greet((dom, lax.rem(band + k, NBAND)))

    @pl.loop(1, NZ)
    def _(k):
        greet((lax.rem(pz + k, NZ) * NX + px, band))

    @pl.loop(1, NX)
    def _(k):
        greet((pz * NX + lax.rem(px + k, NX), band))

    @pl.when(iy == 1)
    def _():
        greet((dom + 2, band))

    @pl.when(iy == 2)
    def _():
        greet((dom - 2, band))

    row, col = iota((PLANE, 128), 0), iota((PLANE, 128), 1)
    ry, rz = row // 16, lax.rem(row, 16)
    cj, cp = lax.rem(col // 16, 2), lax.rem(col, 16)
    one, nil = jnp.float32(1), jnp.float32(0)
    zlo = jnp.where(iz == 0, 14, 0)
    pick[:, 0:128] = jnp.where(jnp.logical_and(ry == cj, rz == cp), one, nil).astype(BF16)
    pick[:, 128:256] = jnp.where(jnp.logical_and(ry == cj + 14, rz == cp), one, nil).astype(BF16)
    pick[:, 256:384] = jnp.where(jnp.logical_and(rz == cj + zlo, ry == cp), one, nil).astype(BF16)

    row, col = iota((PLANE, PLANE), 0), iota((PLANE, PLANE), 1)
    ry, rz, cy, cz = row // 16, lax.rem(row, 16), col // 16, lax.rem(col, 16)
    stencil[0:256, :] = (
        jnp.where(rz == cz, bias(ry - cy), 0.0) + jnp.where(ry == cy, bias(rz - cz), 0.0)
    ).astype(BF16)
    row, col = iota((128, PLANE), 0), iota((128, PLANE), 1)
    cy, cz = col // 16, lax.rem(col, 16)
    rj, rp = lax.rem(row // 16, 2), lax.rem(row, 16)
    stencil[256:384, :] = jnp.where(rp == cz, bias(rj - 2 - cy), 0.0).astype(BF16)
    stencil[384:512, :] = jnp.where(rp == cz, bias(rj + 16 - cy), 0.0).astype(BF16)
    zat = jnp.where(iz == 0, 16, -2)
    stencil[512:640, :] = jnp.where(rp == cy, bias(rj + zat - cz), 0.0).astype(BF16)

    for copy in small:
        copy.wait()

    for i in range(CUBE):
        line = potv[0:1, PLANE * i : PLANE * (i + 1)]
        pterm[16 * i : 16 * i + 16, :] = jnp.broadcast_to(0.25 * (line - 2.25), (16, PLANE))

    for a in range(4):
        where = ptv[a : a + 1, :]
        upper, lower = where // 128, lax.rem(where, 128)
        hot = jnp.where(iota((128, 256), 0) == lower, one, nil).astype(BF16)
        values = projv[a]
        spread = jnp.concatenate(
            [jnp.where(upper == h, values, nil) for h in range(32)], axis=0
        )
        s0, rest = split(spread)
        s1, s2 = split(spread - s0.astype(F32))
        dense = dot(s0, hot, 1, 1) + (dot(s1, hot, 1, 1) + dot(s2, hot, 1, 1))
        flat = jnp.concatenate([dense[8 * h : 8 * h + 8, :] for h in range(32)], axis=1)
        mixed = lax.dot_general(
            0.25 * coupv[a], flat, (((0,), (0,)), ((), ())),
            preferred_element_type=F32, precision=lax.Precision.HIGHEST,
        )
        fh, fl = split(flat)
        eh, el = split(mixed)
        bhl[8 * a : 8 * a + 8, :] = fh.astype(F32)
        bhl[32 + 8 * a : 40 + 8 * a, :] = fl.astype(F32)
        ecat[8 * a : 8 * a + 8, :] = eh.astype(F32)
        ecat[32 + 8 * a : 40 + 8 * a, :] = eh.astype(F32)
        ecat[64 + 8 * a : 72 + 8 * a, :] = el.astype(F32)

    for copy in copies:
        copy.wait()
    pl.semaphore_wait(barrier, 25 + middle.astype(jnp.int32))

    group = iota((64, 128), 1) // 32

    def halo(turn, ref):
        def face(slot, src, dst, where):
            return pltpu.make_async_remote_copy(
                src_ref=src, dst_ref=dst, send_sem=h_send.at[turn, slot],
                recv_sem=h_recv.at[turn, slot], device_id=(where, band), device_id_type=MESH,
            )
        return (
            (iy > 0, iy < 3, face(0, facesend.at[turn, 0], facerecv.at[turn, 1], dom - 2)),
            (iy < 3, iy > 0, face(1, facesend.at[turn, 1], facerecv.at[turn, 0], dom + 2)),
            (None, None, face(2, facesend.at[turn, 2], facerecv.at[turn, 2], dom + 1 - 2 * iz)),
            (ix > 0, ix < 3, face(3, ref.at[pl.ds(32, 32), :], ref.at[pl.ds(288, 32), :], dom - 8)),
            (ix < 3, ix > 0, face(4, ref.at[pl.ds(256, 32), :], ref.at[pl.ds(0, 32), :], dom + 8)),
        )

    def under(condition, action):
        if condition is None:
            action()
        else:
            pl.when(condition)(action)

    def apply(turn, ref):
        faces = halo(turn, ref)
        for slot in (3, 4):
            under(faces[slot][0], faces[slot][2].start)
        here = ref[32:288, :]
        vh, vl = split(here)
        ends = dot(vh, pick[...]) + dot(vl, pick[...])
        for slot in range(3):
            packed = ends[0:64, 128 * slot : 128 * slot + 128]
            for g in range(1, 4):
                packed = jnp.where(
                    group == g, ends[64 * g : 64 * g + 64, 128 * slot : 128 * slot + 128], packed
                )
            facesend[turn, slot] = packed
        for slot in (0, 1, 2):
            under(faces[slot][0], faces[slot][2].start)
        both = jnp.concatenate(
            [jnp.concatenate([v[16 * i : 16 * i + 16, :] for i in range(CUBE)], axis=1) for v in (vh, vl)],
            axis=0,
        )
        quad = dot(both, bhl[...].astype(BF16), 1, 1)
        coef = quad[0:16, 0:32] + (quad[0:16, 32:64] + quad[16:32, 0:32])
        ch, cl = split(coef)
        added = dot(jnp.concatenate([ch, cl, ch], axis=1), ecat[...].astype(BF16))
        added = jnp.concatenate([added[:, PLANE * i : PLANE * (i + 1)] for i in range(CUBE)], axis=0)
        inner = dot(vh, stencil[0:256, :]) + dot(vl, stencil[0:256, :])
        base = pterm[...] * here + added
        for face in faces:
            under(face[1], face[2].wait_recv)
        wide = jnp.concatenate(
            [
                jnp.concatenate(
                    [jnp.where(group == g, facerecv[turn, slot], 0.0) for g in range(4)], axis=0
                )
                for slot in range(3)
            ],
            axis=1,
        )
        wh, wl = split(wide)
        outer = dot(wh, stencil[256:640, :]) + dot(wl, stencil[256:640, :])
        far = ref[0:256, :] + ref[64:320, :]
        near = ref[16:272, :] + ref[48:304, :]
        return base + (1.0 / 96.0) * ((inner + outer) + (far - 16.0 * near))

    vx1[32:288, :] = apply(0, vx0)
    fs[...] = 2.0 * apply(1, vx1) - vx0[32:288, :]

    def to_piece(peer):
        return pltpu.make_async_remote_copy(
            src_ref=fs.at[pl.ds(pl.multiple_of(peer * 16, 16), 16), :],
            dst_ref=work.at[pl.ds(pl.multiple_of(band * 16, 16), 16), pl.ds(PLANE, PLANE)],
            send_sem=a_send.at[peer], recv_sem=a_recv.at[band],
            device_id=(dom, peer), device_id_type=MESH,
        )

    def from_piece(peer):
        return pltpu.make_async_remote_copy(
            src_ref=fs.at[pl.ds(0, 16), :],
            dst_ref=work.at[pl.ds(pl.multiple_of(peer * 16, 16), 16), pl.ds(PLANE, PLANE)],
            send_sem=a_send.at[peer], recv_sem=a_recv.at[peer],
            device_id=(dom, peer), device_id_type=MESH,
        )

    def peers(count, me, action):
        @pl.loop(1, count)
        def _(k):
            action(lax.rem(me + k, count))

    peers(NBAND, band, lambda peer: to_piece(peer).start())
    mine = pl.ds(pl.multiple_of(band * 16, 16), 16)
    work[mine, PLANE : 2 * PLANE] = fs[mine, :]
    peers(NBAND, band, lambda peer: from_piece(peer).wait_recv())

    piece = work[:, PLANE : 2 * PLANE]
    ph, plo = split(piece)
    gram = (1.0 / POINTS) * (dot(ph, ph, 1, 1) + (dot(ph, plo, 1, 1) + dot(plo, ph, 1, 1)))
    row, col = iota((128, 128), 0), iota((128, 128), 1)
    low = gram[128:256, 128:256]
    packed = jnp.where(row >= col, gram[0:128, 0:128], low)
    diag = jnp.sum(jnp.where(row == col, low, 0.0), axis=0, keepdims=True)
    for c in range(NBAND):
        part[c, 0:8, :] = packed[8 * c : 8 * c + 8, :]
        part[c, 8:16, :] = gram[128 + 8 * c : 136 + 8 * c, 0:128]
        part[c, 16:17, :] = diag

    def chunk(src, dst, send, recv, where):
        return pltpu.make_async_remote_copy(
            src_ref=src, dst_ref=dst, send_sem=send, recv_sem=recv, device_id=where, device_id_type=MESH
        )

    def at_band(peer):
        return (dom, peer)

    def at_z(peer):
        return (peer * NX + px, band)

    def at_x(peer):
        return (pz * NX + peer, band)

    def gather(count, me, at, own, buf, send, recv):
        peers(count, me, lambda peer: chunk(
            buf.at[me], buf.at[me], send.at[peer], recv.at[me], at(peer)).start())
        peers(count, me, lambda peer: chunk(
            buf.at[me], buf.at[peer], send.at[peer], recv.at[peer], at(peer)).wait_recv())

    def total(buf, count):
        value = buf[0]
        for i in range(1, count):
            value = value + buf[i]
        return value

    peers(NBAND, band, lambda peer: chunk(
        part.at[peer], rs_buf.at[band], r_send.at[peer], r_recv.at[band], at_band(peer)).start())
    rs_buf[band] = part[band]
    peers(NBAND, band, lambda peer: chunk(
        part.at[peer], rs_buf.at[peer], r_send.at[peer], r_recv.at[peer], at_band(peer)).wait_recv())
    z_buf[pz] = total(rs_buf, NBAND)
    gather(NZ, pz, at_z, None, z_buf, z_send, z_recv)
    x_buf[px] = total(z_buf, NZ)
    gather(NX, px, at_x, None, x_buf, x_send, x_recv)
    g_buf[band] = total(x_buf, NX)
    gather(NBAND, band, at_band, None, g_buf, g_send, g_recv)

    packed = jnp.concatenate([g_buf[c, 0:8, :] for c in range(NBAND)], axis=0)
    cross = jnp.concatenate([g_buf[c, 8:16, :] for c in range(NBAND)], axis=0)
    diag = jnp.broadcast_to(g_buf[0, 16:17, :], (128, 128))
    turned = packed.T
    work[0:128, 0:128] = jnp.where(row >= col, packed, turned)
    work[128:256, 128:256] = jnp.where(row < col, packed, jnp.where(row == col, diag, turned))
    work[128:256, 0:128] = cross
    work[0:128, 128:256] = cross.T

    def to_out(peer):
        return pltpu.make_async_remote_copy(
            src_ref=fs.at[pl.ds(pl.multiple_of(peer * 16, 16), 16), :],
            dst_ref=out.at[:, pl.ds(pl.multiple_of(band * PLANE, PLANE), PLANE)],
            send_sem=o_send.at[peer], recv_sem=o_recv.at[band],
            device_id=(dom, peer), device_id_type=MESH,
        )

    def from_out(peer):
        return pltpu.make_async_remote_copy(
            src_ref=fs.at[pl.ds(0, 16), :],
            dst_ref=out.at[:, pl.ds(pl.multiple_of(peer * PLANE, PLANE), PLANE)],
            send_sem=o_send.at[peer], recv_sem=o_recv.at[peer],
            device_id=(dom, peer), device_id_type=MESH,
        )

    peers(NBAND, band, lambda peer: to_piece(peer).wait_send())

    brow, bcol = iota((BLOCK, 128), 0), iota((BLOCK, 128), 1)
    lane = iota((BLOCK, 256), 1)

    @pl.loop(0, 256 // BLOCK)
    def _(j):
        first = pl.multiple_of(j * BLOCK, BLOCK)
        rows = work[pl.ds(first, BLOCK), :]
        turned = pltpu.roll(rows[:, 0:256], lax.rem(256 + BLOCK - first, 256), 1)
        x = jnp.where(bcol < BLOCK, jnp.where(brow == bcol, 1.0, 0.0), turned[:, 0:128])
        for k in range(BLOCK - 1):
            pivot = x[k : k + 1, :]
            factor = x[:, BLOCK + k : BLOCK + k + 1] * (1.0 / pivot[:, BLOCK + k : BLOCK + k + 1])
            x = x - jnp.where(brow > k, factor, 0.0) * pivot
        d = jnp.sum(jnp.where(bcol == brow + BLOCK, x, 0.0), axis=1, keepdims=True)
        inverse = (x * lax.rsqrt(d))[:, 0:BLOCK]
        done = dot3(inverse, rows)
        fs[pl.ds(first, BLOCK), :] = done[:, 256:512]
        for half in range(BLOCK // 16):
            peer = j * (BLOCK // 16) + half

            @pl.when(peer != band)
            def _():
                to_out(peer).start()

        left = jnp.where(lane >= first + BLOCK, done[:, 0:256], 0.0)
        work[...] = work[...] - dot3(left, done, 0, 0)

    own = pltpu.make_async_copy(
        fs.at[mine, :], out.at[:, pl.ds(pl.multiple_of(band * PLANE, PLANE), PLANE)], o_own
    )
    own.start()
    for turn, ref in ((0, vx0), (1, vx1)):
        for face in halo(turn, ref):
            under(face[0], face[2].wait_send)
    peers(NBAND, band, lambda peer: chunk(
        part.at[peer], rs_buf.at[peer], r_send.at[peer], r_recv.at[peer], at_band(peer)).wait_send())
    for count, me, at, buf, send, recv in (
        (NZ, pz, at_z, z_buf, z_send, z_recv),
        (NX, px, at_x, x_buf, x_send, x_recv),
        (NBAND, band, at_band, g_buf, g_send, g_recv),
    ):
        peers(count, me, lambda peer: chunk(
            buf.at[me], buf.at[peer], send.at[peer], recv.at[peer], at(peer)).wait_send())
    peers(NBAND, band, lambda peer: from_out(peer).wait_recv())
    peers(NBAND, band, lambda peer: to_out(peer).wait_send())
    own.wait()


def local(waves, potential, atom_points, projectors, coupling):
    dma = pltpu.SemaphoreType.DMA
    vmem = pltpu.VMEM
    return pl.pallas_call(
        kernel,
        out_shape=jax.ShapeDtypeStruct((BAND_LOC, CUBE**3), F32),
        in_specs=[pl.BlockSpec(memory_space=pl.ANY)] * 5,
        out_specs=pl.BlockSpec(memory_space=pl.ANY),
        scratch_shapes=[
            vmem((320, 256), F32), vmem((320, 256), F32), vmem((256, 256), F32),
            vmem((2, 3, 64, 128), F32), vmem((2, 3, 64, 128), F32),
            vmem((256, 384), BF16), vmem((640, 256), BF16),
            vmem((64, 4096), F32), vmem((96, 4096), F32),
            vmem((256, 256), F32), vmem((256, 512), F32),
            vmem((4, 256), jnp.int32), vmem((4, 8, 256), F32), vmem((4, 8, 8), F32), vmem((1, 4096), F32),
            vmem((NBAND, ROWS, 128), F32), vmem((NBAND, ROWS, 128), F32),
            vmem((NZ, ROWS, 128), F32), vmem((NX, ROWS, 128), F32), vmem((NBAND, ROWS, 128), F32),
            dma((20,)), dma((2, 5)), dma((2, 5)), dma((16,)), dma((16,)), dma((16,)), dma((16,)),
            dma((8,)), dma((8,)), dma((4,)), dma((4,)), dma((16,)), dma((16,)), dma((16,)), dma((16,)),
            dma,
        ],
        compiler_params=pltpu.CompilerParams(collective_id=0, has_side_effects=True),
    )(waves, potential.reshape(1, CUBE**3), atom_points, projectors, coupling)


def solution(mesh):
    placed = (
        P("band", "dom"),
        P("dom"),
        P("dom", None),
        P("dom", None, None),
        P("dom", None, None),
    )
    return jax.shard_map(
        local, mesh=mesh, in_specs=placed, out_specs=P("band", "dom"), check_vma=False
    )
```

time: 558 us -> 86.5 us (0.16); the launches traced: 549 us -> 86.3 us
  waiting for transfers between devices: 286 us -> 0 us
  other arithmetic: 99.1 us -> 0 us
  Pallas kernels: 0 us -> 84.6 us
  local copies, waits for them, and re-layouts: 69.6 us -> 1.67 us
  starting transfers between devices: 56.5 us -> 0 us
  blocking collectives: 17.7 us -> 0 us
  between operations: 15.7 us -> 0.01 us
    psum x1 -> x0, waiting for transfers between devices: 267 us -> none  [local(): gram = lax.psum(partial_value, ('dom', 'band'))]
    pallas_call x0 -> x1, Pallas kernels: none -> 84.6 us  [local(): pl.pallas_call(kernel, out_shape=jax.ShapeDtypeStruct((BAND_LOC, CUBE **...]
    another operation x10 -> x0, other arithmetic: 53.8 us -> none  [the longest x6 34 us: local(): lower = jnp.linalg.cholesky(gram)]
    ppermute x12 -> x0, starting transfers between devices: 47.3 us -> none  [passed_along(): return lax.ppermute(value, axis, pairs)]
    mul x15 -> x0, other arithmetic: 29 us -> none  [the longest x3 16.2 us: apply_h(): return -0.5 * kinetic + potential[None, :] * values + extra]
    slice x10 -> x0, local copies, waits for them, and re-layouts: 23.3 us -> none  [the longest x8 15.5 us: laplace(): upper_face = lax.slice_in_dim(grid, CUBE - 2, CUBE, axis=axis)]
    mul x6 -> x0, local copies, waits for them, and re-layouts: 19.8 us -> none  [the longest x2 7.73 us: laplace(): shifted(lower_face, -strides[dim])]
    all_to_all x1 -> x0, blocking collectives: 17.7 us -> none  [local(): lax.all_to_all(rotated, 'band', split_axis=0, concat_axis=1, tiled=True)]
  transfers between devices with their start and end apart: 14 -> 0, of which waited for: 3 -> 0; matrix products, arithmetic and copies ran while one was open for 9% -> 0% of each run, Pallas kernels for 0% -> 0%
where the time goes in v1:
time: 86.5 us; the launch traced here: 86.3 us
  Pallas kernels  84.6 us (98%)
  local copies, waits for them, and re-layouts  1.67 us (2%)
    pallas_call x1, Pallas kernels, local(): pl.pallas_call(kernel, out_shape=jax.ShapeDtypeStruct((BAND_LOC, CUBE **...  84.6 us

profile of v1, /device:TPU:1, one launch (start us, length us, event | category | flops | bytes accessed | tf_op | source)
XLA Modules:
  0.0 86.3 jit_solution(17469352346818652794)
XLA Ops:
  0.0 84.6 %shard_map.55 = f32[16,4096]{1,0:T(8,128)} custom-call(f32[16,4096]{1,0:T(8,128)} %waves.1, f32[1,4096]{1,0:T(1,128)} %bitcast.1, s32[4,256]{1,0:T(4,128)} %pts.1, f32[4,8,256]{2,1,0:T(8,128)} %proj.1, f32[4,8,8]{2,1,0:T(8,128)} %coup.1), custom_call_target="tpu_custom_call" | custom-call | tf_op jit(solution)/shard_map/pallas_call | solution.py:380
  84.6 1.7 %copy.7 = f32[16,4096]{1,0:T(8,128)} copy(f32[16,4096]{1,0:T(8,128)} %shard_map.55) | data formatting | bytes 524288

commit v2 on v1

--- a/solution.py
+++ b/solution.py
@@ -326,23 +326,45 @@
 
     peers(NBAND, band, lambda peer: to_piece(peer).wait_send())
 
-    brow, bcol = iota((BLOCK, 128), 0), iota((BLOCK, 128), 1)
-    lane = iota((BLOCK, 256), 1)
-
-    @pl.loop(0, 256 // BLOCK)
-    def _(j):
-        first = pl.multiple_of(j * BLOCK, BLOCK)
-        rows = work[pl.ds(first, BLOCK), :]
-        turned = pltpu.roll(rows[:, 0:256], lax.rem(256 + BLOCK - first, 256), 1)
-        x = jnp.where(bcol < BLOCK, jnp.where(brow == bcol, 1.0, 0.0), turned[:, 0:128])
-        for k in range(BLOCK - 1):
-            pivot = x[k : k + 1, :]
-            factor = x[:, BLOCK + k : BLOCK + k + 1] * (1.0 / pivot[:, BLOCK + k : BLOCK + k + 1])
-            x = x - jnp.where(brow > k, factor, 0.0) * pivot
-        d = jnp.sum(jnp.where(bcol == brow + BLOCK, x, 0.0), axis=1, keepdims=True)
-        inverse = (x * lax.rsqrt(d))[:, 0:BLOCK]
-        done = dot3(inverse, rows)
-        fs[pl.ds(first, BLOCK), :] = done[:, 256:512]
+    srow = iota((8, 128), 0)
+
+    def spread_row(value, k):
+        return jnp.broadcast_to(value[k : k + 1, :], (8, 128))
+
+    for j in range(256 // BLOCK):
+        first = j * BLOCK
+        lo = first // 128 * 128
+        count = BLOCK // 8
+        tiles = [
+            [work[first + 8 * t : first + 8 * t + 8, c : c + 128] for c in range(lo, 512, 128)]
+            for t in range(count)
+        ]
+        for s in range(count):
+            at = first - lo + 8 * s
+            cols = {
+                t: [jnp.broadcast_to(tiles[t][0][:, at + k : at + k + 1], (8, 128)) for k in range(8)]
+                for t in range(s, count)
+            }
+            pivots = cols[s][0]
+            for k in range(8):
+                inverse = 1.0 / spread_row(cols[s][k], k)
+                pivots = jnp.where(srow == k, cols[s][k], pivots)
+                heads = {m: spread_row(cols[s][m], k) for m in range(k + 1, 8)}
+                lead = [spread_row(v, k) for v in tiles[s]]
+                for t in range(s, count):
+                    if t == s and k == 7:
+                        continue
+                    factor = cols[t][k] * inverse
+                    if t == s:
+                        factor = jnp.where(srow > k, factor, 0.0)
+                    for m in range(k + 1, 8):
+                        cols[t][m] = cols[t][m] - factor * heads[m]
+                    tiles[t] = [v - factor * r for v, r in zip(tiles[t], lead)]
+            scale = lax.rsqrt(pivots)
+            tiles[s] = [v * scale for v in tiles[s]]
+        lanes = [jnp.concatenate([tiles[t][c] for t in range(count)], axis=0) for c in range((512 - lo) // 128)]
+        fs[first : first + BLOCK, 0:128] = lanes[-2]
+        fs[first : first + BLOCK, 128:256] = lanes[-1]
         for half in range(BLOCK // 16):
             peer = j * (BLOCK // 16) + half
 
@@ -350,8 +372,13 @@
             def _():
                 to_out(peer).start()
 
-        left = jnp.where(lane >= first + BLOCK, done[:, 0:256], 0.0)
-        work[...] = work[...] - dot3(left, done, 0, 0)
+        after = first + BLOCK
+        if after < 256:
+            base = after // 128 * 128
+            rest = jnp.concatenate(lanes[(base - lo) // 128 :], axis=1)
+            left = rest[:, 0 : 256 - base].T
+            update = dot3(left, rest)
+            work[after:256, base:512] = work[after:256, base:512] - update[after - base :, :]
 
     own = pltpu.make_async_copy(
         fs.at[mine, :], out.at[:, pl.ds(pl.multiple_of(band * PLANE, PLANE), PLANE)], o_own

time: 86.5 us -> 71 us (0.82)
  Pallas kernels: 84.6 us -> 69.1 us
    pallas_call x1, Pallas kernels: 84.6 us -> 69.1 us  [local(): pl.pallas_call(kernel, out_shape=jax.ShapeDtypeStruct((BAND_LOC, CUBE **...]
where the time goes in v2:
time: 71 us; the launch traced here: 70.7 us
  Pallas kernels  69.1 us (97%)
  local copies, waits for them, and re-layouts  1.67 us (2%)
    pallas_call x1, Pallas kernels, local(): pl.pallas_call(kernel, out_shape=jax.ShapeDtypeStruct((BAND_LOC, CUBE **...  69.1 us
    unnamed x1, local copies, waits for them, and re-layouts  1.67 us

profile of v2, /device:TPU:1, one launch (start us, length us, event | category | flops | bytes accessed | tf_op | source)
XLA Modules:
  0.0 70.7 jit_solution(6159510873000917013)
XLA Ops:
  0.0 69.1 %shard_map.55 = f32[16,4096]{1,0:T(8,128)} custom-call(f32[16,4096]{1,0:T(8,128)} %waves.1, f32[1,4096]{1,0:T(1,128)} %bitcast.1, s32[4,256]{1,0:T(4,128)} %pts.1, f32[4,8,256]{2,1,0:T(8,128)} %proj.1, f32[4,8,8]{2,1,0:T(8,128)} %coup.1), custom_call_target="tpu_custom_call" | custom-call | tf_op jit(solution)/shard_map/pallas_call | solution.py:407
  69.1 1.7 %copy.7 = f32[16,4096]{1,0:T(8,128)} copy(f32[16,4096]{1,0:T(8,128)} %shard_map.55) | data formatting | bytes 524288

commit v3 on v2

--- a/solution.py
+++ b/solution.py
@@ -11,8 +11,8 @@
 BAND_LOC = 16
 PLANE = CUBE * CUBE
 POINTS = 131072
-NBAND, NZ, NX = 16, 8, 4
-ROWS = 17
+NBAND, NZ, NY, NX, NSET = 16, 8, 8, 4, 8
+ROWS = 33
 BLOCK = 32
 
 
@@ -29,12 +29,6 @@
     return lax.dot_general(a, b, (((ca,), (cb,)), ((), ())), preferred_element_type=F32)
 
 
-def dot3(a, b, ca=1, cb=0):
-    ah, al = split(a)
-    bh, bl = split(b)
-    return dot(ah, bh, ca, cb) + (dot(ah, bl, ca, cb) + dot(al, bh, ca, cb))
-
-
 def bias(delta):
     step = jnp.abs(delta)
     return jnp.where(step == 1, -16.0, jnp.where(step == 2, 1.0, 0.0))
@@ -43,12 +37,13 @@
 def kernel(
     waves, pot, pts, proj, coup, out,
     vx0, vx1, pterm, facesend, facerecv, pick, stencil, bhl, ecat, fs, work,
-    ptv, projv, coupv, potv, part, rs_buf, z_buf, x_buf, g_buf,
-    in_sem, h_send, h_recv, a_send, a_recv, r_send, r_recv, z_send, z_recv, x_send, x_recv,
-    g_send, g_recv, o_send, o_recv, o_own,
+    ptv, projv, coupv, potv, part, rs_buf, ay_buf, az_buf, bz_buf, by_buf, g_buf,
+    in_sem, h_send, h_recv, a_send, a_recv, r_send, r_recv, s_send, s_recv, o_send, o_recv, o_own,
 ):
     dom, band = lax.axis_index("dom"), lax.axis_index("band")
     pz, px = dom // NX, lax.rem(dom, NX)
+    py, core = band // 2, lax.rem(band, 2)
+    mine_set = px * 2 + core
     iz = lax.rem(dom, 2)
     iy = lax.rem(dom // 2, 4)
     ix = dom // 8
@@ -72,6 +67,18 @@
         ref[0:32, :] = jnp.zeros((32, PLANE), F32)
         ref[288:320, :] = jnp.zeros((32, PLANE), F32)
 
+    def at_band(peer):
+        return (dom, peer)
+
+    def at_y(peer):
+        return (dom, peer * 2 + core)
+
+    def at_z(peer):
+        return (peer * NX + px, band)
+
+    def at_set(peer):
+        return (pz * NX + peer // 2, py * 2 + lax.rem(peer, 2))
+
     barrier = pltpu.get_barrier_semaphore()
 
     def greet(where):
@@ -85,9 +92,9 @@
     def _(k):
         greet((lax.rem(pz + k, NZ) * NX + px, band))
 
-    @pl.loop(1, NX)
+    @pl.loop(1, NSET)
     def _(k):
-        greet((pz * NX + lax.rem(px + k, NX), band))
+        greet(at_set(lax.rem(mine_set + k, NSET)))
 
     @pl.when(iy == 1)
     def _():
@@ -97,64 +104,7 @@
     def _():
         greet((dom - 2, band))
 
-    row, col = iota((PLANE, 128), 0), iota((PLANE, 128), 1)
-    ry, rz = row // 16, lax.rem(row, 16)
-    cj, cp = lax.rem(col // 16, 2), lax.rem(col, 16)
-    one, nil = jnp.float32(1), jnp.float32(0)
-    zlo = jnp.where(iz == 0, 14, 0)
-    pick[:, 0:128] = jnp.where(jnp.logical_and(ry == cj, rz == cp), one, nil).astype(BF16)
-    pick[:, 128:256] = jnp.where(jnp.logical_and(ry == cj + 14, rz == cp), one, nil).astype(BF16)
-    pick[:, 256:384] = jnp.where(jnp.logical_and(rz == cj + zlo, ry == cp), one, nil).astype(BF16)
-
-    row, col = iota((PLANE, PLANE), 0), iota((PLANE, PLANE), 1)
-    ry, rz, cy, cz = row // 16, lax.rem(row, 16), col // 16, lax.rem(col, 16)
-    stencil[0:256, :] = (
-        jnp.where(rz == cz, bias(ry - cy), 0.0) + jnp.where(ry == cy, bias(rz - cz), 0.0)
-    ).astype(BF16)
-    row, col = iota((128, PLANE), 0), iota((128, PLANE), 1)
-    cy, cz = col // 16, lax.rem(col, 16)
-    rj, rp = lax.rem(row // 16, 2), lax.rem(row, 16)
-    stencil[256:384, :] = jnp.where(rp == cz, bias(rj - 2 - cy), 0.0).astype(BF16)
-    stencil[384:512, :] = jnp.where(rp == cz, bias(rj + 16 - cy), 0.0).astype(BF16)
-    zat = jnp.where(iz == 0, 16, -2)
-    stencil[512:640, :] = jnp.where(rp == cy, bias(rj + zat - cz), 0.0).astype(BF16)
-
-    for copy in small:
-        copy.wait()
-
-    for i in range(CUBE):
-        line = potv[0:1, PLANE * i : PLANE * (i + 1)]
-        pterm[16 * i : 16 * i + 16, :] = jnp.broadcast_to(0.25 * (line - 2.25), (16, PLANE))
-
-    for a in range(4):
-        where = ptv[a : a + 1, :]
-        upper, lower = where // 128, lax.rem(where, 128)
-        hot = jnp.where(iota((128, 256), 0) == lower, one, nil).astype(BF16)
-        values = projv[a]
-        spread = jnp.concatenate(
-            [jnp.where(upper == h, values, nil) for h in range(32)], axis=0
-        )
-        s0, rest = split(spread)
-        s1, s2 = split(spread - s0.astype(F32))
-        dense = dot(s0, hot, 1, 1) + (dot(s1, hot, 1, 1) + dot(s2, hot, 1, 1))
-        flat = jnp.concatenate([dense[8 * h : 8 * h + 8, :] for h in range(32)], axis=1)
-        mixed = lax.dot_general(
-            0.25 * coupv[a], flat, (((0,), (0,)), ((), ())),
-            preferred_element_type=F32, precision=lax.Precision.HIGHEST,
-        )
-        fh, fl = split(flat)
-        eh, el = split(mixed)
-        bhl[8 * a : 8 * a + 8, :] = fh.astype(F32)
-        bhl[32 + 8 * a : 40 + 8 * a, :] = fl.astype(F32)
-        ecat[8 * a : 8 * a + 8, :] = eh.astype(F32)
-        ecat[32 + 8 * a : 40 + 8 * a, :] = eh.astype(F32)
-        ecat[64 + 8 * a : 72 + 8 * a, :] = el.astype(F32)
-
-    for copy in copies:
-        copy.wait()
-    pl.semaphore_wait(barrier, 25 + middle.astype(jnp.int32))
-
-    group = iota((64, 128), 1) // 32
+    group = iota((64, 128), 1) >> 5
 
     def halo(turn, ref):
         def face(slot, src, dst, where):
@@ -176,12 +126,8 @@
         else:
             pl.when(condition)(action)
 
-    def apply(turn, ref):
-        faces = halo(turn, ref)
-        for slot in (3, 4):
-            under(faces[slot][0], faces[slot][2].start)
-        here = ref[32:288, :]
-        vh, vl = split(here)
+    def pack_faces(turn, ref):
+        vh, vl = split(ref[32:288, :])
         ends = dot(vh, pick[...]) + dot(vl, pick[...])
         for slot in range(3):
             packed = ends[0:64, 128 * slot : 128 * slot + 128]
@@ -190,8 +136,15 @@
                     group == g, ends[64 * g : 64 * g + 64, 128 * slot : 128 * slot + 128], packed
                 )
             facesend[turn, slot] = packed
-        for slot in (0, 1, 2):
+
+    def send_faces(turn, ref, slots):
+        faces = halo(turn, ref)
+        for slot in slots:
             under(faces[slot][0], faces[slot][2].start)
+
+    def inside(ref):
+        here = ref[32:288, :]
+        vh, vl = split(here)
         both = jnp.concatenate(
             [jnp.concatenate([v[16 * i : 16 * i + 16, :] for i in range(CUBE)], axis=1) for v in (vh, vl)],
             axis=0,
@@ -202,8 +155,10 @@
         added = dot(jnp.concatenate([ch, cl, ch], axis=1), ecat[...].astype(BF16))
         added = jnp.concatenate([added[:, PLANE * i : PLANE * (i + 1)] for i in range(CUBE)], axis=0)
         inner = dot(vh, stencil[0:256, :]) + dot(vl, stencil[0:256, :])
-        base = pterm[...] * here + added
-        for face in faces:
+        return pterm[...] * here + added + (1.0 / 96.0) * inner
+
+    def outside(turn, ref):
+        for face in halo(turn, ref):
             under(face[1], face[2].wait_recv)
         wide = jnp.concatenate(
             [
@@ -218,10 +173,72 @@
         outer = dot(wh, stencil[256:640, :]) + dot(wl, stencil[256:640, :])
         far = ref[0:256, :] + ref[64:320, :]
         near = ref[16:272, :] + ref[48:304, :]
-        return base + (1.0 / 96.0) * ((inner + outer) + (far - 16.0 * near))
-
-    vx1[32:288, :] = apply(0, vx0)
-    fs[...] = 2.0 * apply(1, vx1) - vx0[32:288, :]
+        return (1.0 / 96.0) * (outer + (far - 16.0 * near))
+
+    row, col = iota((PLANE, 128), 0), iota((PLANE, 128), 1)
+    ry, rz = row >> 4, row & 15
+    cj, cp = (col >> 4) & 1, col & 15
+    one, nil = jnp.float32(1), jnp.float32(0)
+    zlo = jnp.where(iz == 0, 14, 0)
+    pick[:, 0:128] = jnp.where(row == (col & 31), one, nil).astype(BF16)
+    pick[:, 128:256] = jnp.where(row == (col & 31) + 224, one, nil).astype(BF16)
+    pick[:, 256:384] = jnp.where(row == cp * 16 + cj + zlo, one, nil).astype(BF16)
+
+    for copy in copies:
+        copy.wait()
+    pack_faces(0, vx0)
+    pl.semaphore_wait(barrier, 29 + middle.astype(jnp.int32))
+    send_faces(0, vx0, range(5))
+
+    row, col = iota((PLANE, PLANE), 0), iota((PLANE, PLANE), 1)
+    ry, rz, cy, cz = row >> 4, row & 15, col >> 4, col & 15
+    stencil[0:256, :] = (
+        jnp.where(rz == cz, bias(ry - cy), 0.0) + jnp.where(ry == cy, bias(rz - cz), 0.0)
+    ).astype(BF16)
+    row, col = iota((128, PLANE), 0), iota((128, PLANE), 1)
+    cy, cz = col >> 4, col & 15
+    rj, rp = (row >> 4) & 1, row & 15
+    stencil[256:384, :] = jnp.where(rp == cz, bias(rj - 2 - cy), 0.0).astype(BF16)
+    stencil[384:512, :] = jnp.where(rp == cz, bias(rj + 16 - cy), 0.0).astype(BF16)
+    zat = jnp.where(iz == 0, 16, -2)
+    stencil[512:640, :] = jnp.where(rp == cy, bias(rj + zat - cz), 0.0).astype(BF16)
+
+    for copy in small:
+        copy.wait()
+
+    for i in range(CUBE):
+        line = potv[0:1, PLANE * i : PLANE * (i + 1)]
+        pterm[16 * i : 16 * i + 16, :] = jnp.broadcast_to(0.25 * (line - 2.25), (16, PLANE))
+
+    for a in range(4):
+        where = ptv[a : a + 1, :]
+        upper, lower = where >> 7, where & 127
+        hot = jnp.where(iota((128, 256), 0) == lower, one, nil).astype(BF16)
+        values = projv[a]
+        spread = jnp.concatenate(
+            [jnp.where(upper == h, values, nil) for h in range(32)], axis=0
+        )
+        s0, rest = split(spread)
+        s1, s2 = split(spread - s0.astype(F32))
+        dense = dot(s0, hot, 1, 1) + (dot(s1, hot, 1, 1) + dot(s2, hot, 1, 1))
+        flat = jnp.concatenate([dense[8 * h : 8 * h + 8, :] for h in range(32)], axis=1)
+        mixed = lax.dot_general(
+            0.25 * coupv[a], flat, (((0,), (0,)), ((), ())),
+            preferred_element_type=F32, precision=lax.Precision.HIGHEST,
+        )
+        fh, fl = split(flat)
+        eh, el = split(mixed)
+        bhl[8 * a : 8 * a + 8, :] = fh.astype(F32)
+        bhl[32 + 8 * a : 40 + 8 * a, :] = fl.astype(F32)
+        ecat[8 * a : 8 * a + 8, :] = eh.astype(F32)
+        ecat[32 + 8 * a : 40 + 8 * a, :] = eh.astype(F32)
+        ecat[64 + 8 * a : 72 + 8 * a, :] = el.astype(F32)
+
+    vx1[32:288, :] = inside(vx0) + outside(0, vx0)
+    send_faces(1, vx1, (3, 4))
+    pack_faces(1, vx1)
+    send_faces(1, vx1, range(3))
+    fs[...] = 2.0 * (inside(vx1) + outside(1, vx1)) - vx0[32:288, :]
 
     def to_piece(peer):
         return pltpu.make_async_remote_copy(
@@ -240,9 +257,10 @@
         )
 
     def peers(count, me, action):
-        @pl.loop(1, count)
+        @pl.loop(0, count - 1)
         def _(k):
-            action(lax.rem(me + k, count))
+            step = count // 2 + (1 - 2 * lax.rem(k, 2)) * ((k + 1) // 2)
+            action(lax.rem(me + step, count))
 
     peers(NBAND, band, lambda peer: to_piece(peer).start())
     mine = pl.ds(pl.multiple_of(band * 16, 16), 16)
@@ -256,30 +274,27 @@
     low = gram[128:256, 128:256]
     packed = jnp.where(row >= col, gram[0:128, 0:128], low)
     diag = jnp.sum(jnp.where(row == col, low, 0.0), axis=0, keepdims=True)
-    for c in range(NBAND):
-        part[c, 0:8, :] = packed[8 * c : 8 * c + 8, :]
-        part[c, 8:16, :] = gram[128 + 8 * c : 136 + 8 * c, 0:128]
-        part[c, 16:17, :] = diag
+    for c in range(NSET):
+        part[c, 0:16, :] = packed[16 * c : 16 * c + 16, :]
+        part[c, 16:32, :] = gram[128 + 16 * c : 144 + 16 * c, 0:128]
+        part[c, 32:33, :] = diag
 
     def chunk(src, dst, send, recv, where):
         return pltpu.make_async_remote_copy(
             src_ref=src, dst_ref=dst, send_sem=send, recv_sem=recv, device_id=where, device_id_type=MESH
         )
 
-    def at_band(peer):
-        return (dom, peer)
-
-    def at_z(peer):
-        return (peer * NX + px, band)
-
-    def at_x(peer):
-        return (pz * NX + peer, band)
-
-    def gather(count, me, at, own, buf, send, recv):
+    def share(count, me, at, buf, send, recv):
         peers(count, me, lambda peer: chunk(
             buf.at[me], buf.at[me], send.at[peer], recv.at[me], at(peer)).start())
+
+    def collect(count, me, at, buf, send, recv):
         peers(count, me, lambda peer: chunk(
             buf.at[me], buf.at[peer], send.at[peer], recv.at[peer], at(peer)).wait_recv())
+
+    def drain(count, me, at, buf, send, recv):
+        peers(count, me, lambda peer: chunk(
+            buf.at[me], buf.at[peer], send.at[peer], recv.at[peer], at(peer)).wait_send())
 
     def total(buf, count):
         value = buf[0]
@@ -287,21 +302,37 @@
             value = value + buf[i]
         return value
 
-    peers(NBAND, band, lambda peer: chunk(
-        part.at[peer], rs_buf.at[band], r_send.at[peer], r_recv.at[band], at_band(peer)).start())
-    rs_buf[band] = part[band]
-    peers(NBAND, band, lambda peer: chunk(
-        part.at[peer], rs_buf.at[peer], r_send.at[peer], r_recv.at[peer], at_band(peer)).wait_recv())
-    z_buf[pz] = total(rs_buf, NBAND)
-    gather(NZ, pz, at_z, None, z_buf, z_send, z_recv)
-    x_buf[px] = total(z_buf, NZ)
-    gather(NX, px, at_x, None, x_buf, x_send, x_recv)
-    g_buf[band] = total(x_buf, NX)
-    gather(NBAND, band, at_band, None, g_buf, g_send, g_recv)
-
-    packed = jnp.concatenate([g_buf[c, 0:8, :] for c in range(NBAND)], axis=0)
-    cross = jnp.concatenate([g_buf[c, 8:16, :] for c in range(NBAND)], axis=0)
-    diag = jnp.broadcast_to(g_buf[0, 16:17, :], (128, 128))
+    peers(NSET, mine_set, lambda peer: chunk(
+        part.at[peer], rs_buf.at[mine_set], r_send.at[peer], r_recv.at[mine_set], at_set(peer)).start())
+    rs_buf[mine_set] = part[mine_set]
+    peers(NSET, mine_set, lambda peer: chunk(
+        part.at[peer], rs_buf.at[peer], r_send.at[peer], r_recv.at[peer], at_set(peer)).wait_recv())
+    value = total(rs_buf, NSET)
+    a_y = (NY, py, at_y, ay_buf, s_send.at[0], s_recv.at[0])
+    b_z = (NZ, pz, at_z, bz_buf, s_send.at[1], s_recv.at[1])
+    a_z = (NZ, pz, at_z, az_buf, s_send.at[2], s_recv.at[2])
+    b_y = (NY, py, at_y, by_buf, s_send.at[3], s_recv.at[3])
+    a_set = (NSET, mine_set, at_set, g_buf, s_send.at[4], s_recv.at[4])
+    ay_buf[py] = value[0:16]
+    share(*a_y)
+    bz_buf[pz] = value[16:33]
+    share(*b_z)
+    collect(*a_y)
+    az_buf[pz] = total(ay_buf, NY)
+    share(*a_z)
+    collect(*b_z)
+    by_buf[py] = total(bz_buf, NZ)
+    share(*b_y)
+    collect(*a_z)
+    g_buf[mine_set, 0:16, :] = total(az_buf, NZ)
+    collect(*b_y)
+    g_buf[mine_set, 16:33, :] = total(by_buf, NY)
+    share(*a_set)
+    collect(*a_set)
+
+    packed = jnp.concatenate([g_buf[c, 0:16, :] for c in range(NSET)], axis=0)
+    cross = jnp.concatenate([g_buf[c, 16:32, :] for c in range(NSET)], axis=0)
+    diag = jnp.broadcast_to(g_buf[0, 32:33, :], (128, 128))
     turned = packed.T
     work[0:128, 0:128] = jnp.where(row >= col, packed, turned)
     work[128:256, 128:256] = jnp.where(row < col, packed, jnp.where(row == col, diag, turned))
@@ -376,9 +407,13 @@
         if after < 256:
             base = after // 128 * 128
             rest = jnp.concatenate(lanes[(base - lo) // 128 :], axis=1)
-            left = rest[:, 0 : 256 - base].T
-            update = dot3(left, rest)
-            work[after:256, base:512] = work[after:256, base:512] - update[after - base :, :]
+            high, low = split(rest)
+            lead = high[:, 0 : 256 - base].astype(F32)
+            left = jnp.concatenate([lead, lead, rest[:, 0 : 256 - base] - lead], axis=0).T
+            left = left[after - base :, :].astype(BF16)
+            work[after:256, base:512] = work[after:256, base:512] - dot(
+                left, jnp.concatenate([high, low, high], axis=0)
+            )
 
     own = pltpu.make_async_copy(
         fs.at[mine, :], out.at[:, pl.ds(pl.multiple_of(band * PLANE, PLANE), PLANE)], o_own
@@ -387,15 +422,10 @@
     for turn, ref in ((0, vx0), (1, vx1)):
         for face in halo(turn, ref):
             under(face[0], face[2].wait_send)
-    peers(NBAND, band, lambda peer: chunk(
-        part.at[peer], rs_buf.at[peer], r_send.at[peer], r_recv.at[peer], at_band(peer)).wait_send())
-    for count, me, at, buf, send, recv in (
-        (NZ, pz, at_z, z_buf, z_send, z_recv),
-        (NX, px, at_x, x_buf, x_send, x_recv),
-        (NBAND, band, at_band, g_buf, g_send, g_recv),
-    ):
-        peers(count, me, lambda peer: chunk(
-            buf.at[me], buf.at[peer], send.at[peer], recv.at[peer], at(peer)).wait_send())
+    peers(NSET, mine_set, lambda peer: chunk(
+        part.at[peer], rs_buf.at[peer], r_send.at[peer], r_recv.at[peer], at_set(peer)).wait_send())
+    for stage in (a_y, b_z, a_z, b_y, a_set):
+        drain(*stage)
     peers(NBAND, band, lambda peer: from_out(peer).wait_recv())
     peers(NBAND, band, lambda peer: to_out(peer).wait_send())
     own.wait()
@@ -416,11 +446,11 @@
             vmem((64, 4096), F32), vmem((96, 4096), F32),
             vmem((256, 256), F32), vmem((256, 512), F32),
             vmem((4, 256), jnp.int32), vmem((4, 8, 256), F32), vmem((4, 8, 8), F32), vmem((1, 4096), F32),
-            vmem((NBAND, ROWS, 128), F32), vmem((NBAND, ROWS, 128), F32),
-            vmem((NZ, ROWS, 128), F32), vmem((NX, ROWS, 128), F32), vmem((NBAND, ROWS, 128), F32),
-            dma((20,)), dma((2, 5)), dma((2, 5)), dma((16,)), dma((16,)), dma((16,)), dma((16,)),
-            dma((8,)), dma((8,)), dma((4,)), dma((4,)), dma((16,)), dma((16,)), dma((16,)), dma((16,)),
-            dma,
+            vmem((NSET, ROWS, 128), F32), vmem((NSET, ROWS, 128), F32),
+            vmem((NY, 16, 128), F32), vmem((NZ, 16, 128), F32),
+            vmem((NZ, 17, 128), F32), vmem((NY, 17, 128), F32), vmem((NSET, ROWS, 128), F32),
+            dma((20,)), dma((2, 5)), dma((2, 5)), dma((16,)), dma((16,)), dma((8,)), dma((8,)),
+            dma((5, 8)), dma((5, 8)), dma((16,)), dma((16,)), dma,
         ],
         compiler_params=pltpu.CompilerParams(collective_id=0, has_side_effects=True),
     )(waves, potential.reshape(1, CUBE**3), atom_points, projectors, coupling)

time: 71 us -> 65.3 us (0.920)
  Pallas kernels: 69.1 us -> 63.3 us
    pallas_call x1, Pallas kernels: 69.1 us -> 63.3 us  [local(): pl.pallas_call(kernel, out_shape=jax.ShapeDtypeStruct((BAND_LOC, CUBE **...]
where the time goes in v3:
time: 65.3 us; the launch traced here: 64.9 us
  Pallas kernels  63.3 us (97%)
  local copies, waits for them, and re-layouts  1.67 us (3%)
    pallas_call x1, Pallas kernels, local(): pl.pallas_call(kernel, out_shape=jax.ShapeDtypeStruct((BAND_LOC, CUBE **...  63.3 us
    unnamed x1, local copies, waits for them, and re-layouts  1.67 us

profile of v3, /device:TPU:1, one launch (start us, length us, event | category | flops | bytes accessed | tf_op | source)
XLA Modules:
  0.0 64.9 jit_solution(8806560769218298611)
XLA Ops:
  0.0 63.3 %shard_map.55 = f32[16,4096]{1,0:T(8,128)} custom-call(f32[16,4096]{1,0:T(8,128)} %waves.1, f32[1,4096]{1,0:T(1,128)} %bitcast.1, s32[4,256]{1,0:T(4,128)} %pts.1, f32[4,8,256]{2,1,0:T(8,128)} %proj.1, f32[4,8,8]{2,1,0:T(8,128)} %coup.1), custom_call_target="tpu_custom_call" | custom-call | tf_op jit(solution)/shard_map/pallas_call | solution.py:437
  63.3 1.7 %copy.7 = f32[16,4096]{1,0:T(8,128)} copy(f32[16,4096]{1,0:T(8,128)} %shard_map.55) | data formatting | bytes 524288

commit v4 on v3

--- a/solution.py
+++ b/solution.py
@@ -36,7 +36,7 @@
 
 def kernel(
     waves, pot, pts, proj, coup, out,
-    vx0, vx1, pterm, facesend, facerecv, pick, stencil, bhl, ecat, fs, work,
+    vx0, vx1, pterm, facesend, facerecv, pick, stencil, bcat, couple, fs, work,
     ptv, projv, coupv, potv, part, rs_buf, ay_buf, az_buf, bz_buf, by_buf, g_buf,
     in_sem, h_send, h_recv, a_send, a_recv, r_send, r_recv, s_send, s_recv, o_send, o_recv, o_own,
 ):
@@ -63,6 +63,7 @@
         copy.start()
 
     facerecv[...] = jnp.zeros_like(facerecv)
+    couple[...] = jnp.zeros_like(couple)
     for ref in (vx0, vx1):
         ref[0:32, :] = jnp.zeros((32, PLANE), F32)
         ref[288:320, :] = jnp.zeros((32, PLANE), F32)
@@ -126,16 +127,23 @@
         else:
             pl.when(condition)(action)
 
-    def pack_faces(turn, ref):
+    def pack_y(turn, ref):
+        for slot, at in ((0, 0), (1, 128)):
+            packed = None
+            for g in range(4):
+                shift = (32 * g + 32 * slot) % 128
+                part = ref[32 + 64 * g : 96 + 64 * g, at : at + 128]
+                part = pltpu.roll(part, shift, 1) if shift else part
+                packed = part if g == 0 else jnp.where(group == g, part, packed)
+            facesend[turn, slot] = packed
+
+    def pack_z(turn, ref):
         vh, vl = split(ref[32:288, :])
         ends = dot(vh, pick[...]) + dot(vl, pick[...])
-        for slot in range(3):
-            packed = ends[0:64, 128 * slot : 128 * slot + 128]
-            for g in range(1, 4):
-                packed = jnp.where(
-                    group == g, ends[64 * g : 64 * g + 64, 128 * slot : 128 * slot + 128], packed
-                )
-            facesend[turn, slot] = packed
+        packed = ends[0:64, :]
+        for g in range(1, 4):
+            packed = jnp.where(group == g, ends[64 * g : 64 * g + 64, :], packed)
+        facesend[turn, 2] = packed
 
     def send_faces(turn, ref, slots):
         faces = halo(turn, ref)
@@ -149,10 +157,12 @@
             [jnp.concatenate([v[16 * i : 16 * i + 16, :] for i in range(CUBE)], axis=1) for v in (vh, vl)],
             axis=0,
         )
-        quad = dot(both, bhl[...].astype(BF16), 1, 1)
+        quad = dot(both, bcat[0:64, :], 1, 1)
         coef = quad[0:16, 0:32] + (quad[0:16, 32:64] + quad[16:32, 0:32])
         ch, cl = split(coef)
-        added = dot(jnp.concatenate([ch, cl, ch], axis=1), ecat[...].astype(BF16))
+        kh, kl = split(couple[...])
+        ch, cl = split(dot(ch, kh, 1, 1) + (dot(ch, kl, 1, 1) + dot(cl, kh, 1, 1)))
+        added = dot(jnp.concatenate([ch, ch, cl], axis=1), bcat[...])
         added = jnp.concatenate([added[:, PLANE * i : PLANE * (i + 1)] for i in range(CUBE)], axis=0)
         inner = dot(vh, stencil[0:256, :]) + dot(vl, stencil[0:256, :])
         return pterm[...] * here + added + (1.0 / 96.0) * inner
@@ -180,13 +190,12 @@
     cj, cp = (col >> 4) & 1, col & 15
     one, nil = jnp.float32(1), jnp.float32(0)
     zlo = jnp.where(iz == 0, 14, 0)
-    pick[:, 0:128] = jnp.where(row == (col & 31), one, nil).astype(BF16)
-    pick[:, 128:256] = jnp.where(row == (col & 31) + 224, one, nil).astype(BF16)
-    pick[:, 256:384] = jnp.where(row == cp * 16 + cj + zlo, one, nil).astype(BF16)
+    pick[...] = jnp.where(row == cp * 16 + cj + zlo, one, nil).astype(BF16)
 
     for copy in copies:
         copy.wait()
-    pack_faces(0, vx0)
+    pack_y(0, vx0)
+    pack_z(0, vx0)
     pl.semaphore_wait(barrier, 29 + middle.astype(jnp.int32))
     send_faces(0, vx0, range(5))
 
@@ -210,34 +219,36 @@
         line = potv[0:1, PLANE * i : PLANE * (i + 1)]
         pterm[16 * i : 16 * i + 16, :] = jnp.broadcast_to(0.25 * (line - 2.25), (16, PLANE))
 
-    for a in range(4):
-        where = ptv[a : a + 1, :]
-        upper, lower = where >> 7, where & 127
-        hot = jnp.where(iota((128, 256), 0) == lower, one, nil).astype(BF16)
-        values = projv[a]
-        spread = jnp.concatenate(
-            [jnp.where(upper == h, values, nil) for h in range(32)], axis=0
-        )
-        s0, rest = split(spread)
-        s1, s2 = split(spread - s0.astype(F32))
-        dense = dot(s0, hot, 1, 1) + (dot(s1, hot, 1, 1) + dot(s2, hot, 1, 1))
-        flat = jnp.concatenate([dense[8 * h : 8 * h + 8, :] for h in range(32)], axis=1)
-        mixed = lax.dot_general(
-            0.25 * coupv[a], flat, (((0,), (0,)), ((), ())),
-            preferred_element_type=F32, precision=lax.Precision.HIGHEST,
-        )
-        fh, fl = split(flat)
-        eh, el = split(mixed)
-        bhl[8 * a : 8 * a + 8, :] = fh.astype(F32)
-        bhl[32 + 8 * a : 40 + 8 * a, :] = fl.astype(F32)
-        ecat[8 * a : 8 * a + 8, :] = eh.astype(F32)
-        ecat[32 + 8 * a : 40 + 8 * a, :] = eh.astype(F32)
-        ecat[64 + 8 * a : 72 + 8 * a, :] = el.astype(F32)
+    for pair in range(2):
+        flats = []
+        for a in (2 * pair, 2 * pair + 1):
+            where = ptv[a : a + 1, :]
+            upper, lower = where >> 7, where & 127
+            hot = jnp.where(iota((128, 256), 0) == lower, one, nil).astype(BF16)
+            values = projv[a]
+            lead = values.astype(BF16).astype(F32)
+            parts = jnp.concatenate([lead, values - lead], axis=0)
+            spread = jnp.concatenate(
+                [jnp.where(upper == h, parts, nil).astype(BF16) for h in range(32)], axis=0
+            )
+            dense = dot(spread, hot, 1, 1)
+            flats.append(
+                [dense[16 * h : 16 * h + 8, :] + dense[16 * h + 8 : 16 * h + 16, :] for h in range(32)]
+            )
+            couple[8 * a : 8 * a + 8, 8 * a : 8 * a + 8] = 0.25 * coupv[a]
+        for h in range(32):
+            fh, fl = split(jnp.concatenate([flats[0][h], flats[1][h]], axis=0))
+            here = slice(128 * h, 128 * h + 128)
+            bcat[16 * pair : 16 * pair + 16, here] = fh
+            bcat[32 + 16 * pair : 48 + 16 * pair, here] = fl
+            bcat[64 + 16 * pair : 80 + 16 * pair, here] = fh
 
     vx1[32:288, :] = inside(vx0) + outside(0, vx0)
     send_faces(1, vx1, (3, 4))
-    pack_faces(1, vx1)
-    send_faces(1, vx1, range(3))
+    pack_y(1, vx1)
+    send_faces(1, vx1, (0, 1))
+    pack_z(1, vx1)
+    send_faces(1, vx1, (2,))
     fs[...] = 2.0 * (inside(vx1) + outside(1, vx1)) - vx0[32:288, :]
 
     def to_piece(peer):
@@ -370,27 +381,46 @@
             [work[first + 8 * t : first + 8 * t + 8, c : c + 128] for c in range(lo, 512, 128)]
             for t in range(count)
         ]
+
+        def columns(s, start):
+            at = first - lo + 8 * s
+            return {
+                t: [jnp.broadcast_to(tiles[t][0][:, at + k : at + k + 1], (8, 128)) for k in range(8)]
+                for t in range(start, count)
+            }
+
+        cols = columns(0, 0)
         for s in range(count):
-            at = first - lo + 8 * s
-            cols = {
-                t: [jnp.broadcast_to(tiles[t][0][:, at + k : at + k + 1], (8, 128)) for k in range(8)]
-                for t in range(s, count)
-            }
-            pivots = cols[s][0]
+            coming = columns(s + 1, s) if s + 1 < count else None
+            factors = []
+            pivot = spread_row(cols[s][0], 0)
+            pivots = pivot
             for k in range(8):
-                inverse = 1.0 / spread_row(cols[s][k], k)
-                pivots = jnp.where(srow == k, cols[s][k], pivots)
+                inverse = 1.0 / pivot
                 heads = {m: spread_row(cols[s][m], k) for m in range(k + 1, 8)}
                 lead = [spread_row(v, k) for v in tiles[s]]
-                for t in range(s, count):
-                    if t == s and k == 7:
-                        continue
-                    factor = cols[t][k] * inverse
-                    if t == s:
-                        factor = jnp.where(srow > k, factor, 0.0)
+                if k < 7:
+                    pivot = spread_row(cols[s][k + 1], k + 1) - (
+                        spread_row(cols[s][k], k + 1) * inverse
+                    ) * heads[k + 1]
+                    pivots = jnp.where(srow > k, pivot, pivots)
+                factor = {
+                    t: (jnp.where(srow > k, cols[s][k], 0.0) if t == s else cols[t][k]) * inverse
+                    for t in range(s, count)
+                    if t != s or k < 7
+                }
+                factors.append(factor)
+                for t in factor:
                     for m in range(k + 1, 8):
-                        cols[t][m] = cols[t][m] - factor * heads[m]
-                    tiles[t] = [v - factor * r for v, r in zip(tiles[t], lead)]
+                        cols[t][m] = cols[t][m] - factor[t] * heads[m]
+                    tiles[t] = [v - factor[t] * r for v, r in zip(tiles[t], lead)]
+            if coming is not None:
+                for k in range(8):
+                    heads = [spread_row(coming[s][m], k) for m in range(8)]
+                    for t in factors[k]:
+                        for m in range(8):
+                            coming[t][m] = coming[t][m] - factors[k][t] * heads[m]
+                cols = coming
             scale = lax.rsqrt(pivots)
             tiles[s] = [v * scale for v in tiles[s]]
         lanes = [jnp.concatenate([tiles[t][c] for t in range(count)], axis=0) for c in range((512 - lo) // 128)]
@@ -437,13 +467,13 @@
     return pl.pallas_call(
         kernel,
         out_shape=jax.ShapeDtypeStruct((BAND_LOC, CUBE**3), F32),
-        in_specs=[pl.BlockSpec(memory_space=pl.ANY)] * 5,
+        in_specs=[pl.BlockSpec(memory_space=pltpu.MemorySpace.HBM)] * 5,
         out_specs=pl.BlockSpec(memory_space=pl.ANY),
         scratch_shapes=[
             vmem((320, 256), F32), vmem((320, 256), F32), vmem((256, 256), F32),
             vmem((2, 3, 64, 128), F32), vmem((2, 3, 64, 128), F32),
-            vmem((256, 384), BF16), vmem((640, 256), BF16),
-            vmem((64, 4096), F32), vmem((96, 4096), F32),
+            vmem((256, 128), BF16), vmem((640, 256), BF16),
+            vmem((96, 4096), BF16), vmem((32, 32), F32),
             vmem((256, 256), F32), vmem((256, 512), F32),
             vmem((4, 256), jnp.int32), vmem((4, 8, 256), F32), vmem((4, 8, 8), F32), vmem((1, 4096), F32),
             vmem((NSET, ROWS, 128), F32), vmem((NSET, ROWS, 128), F32),
@@ -452,8 +482,13 @@
             dma((20,)), dma((2, 5)), dma((2, 5)), dma((16,)), dma((16,)), dma((8,)), dma((8,)),
             dma((5, 8)), dma((5, 8)), dma((16,)), dma((16,)), dma,
         ],
-        compiler_params=pltpu.CompilerParams(collective_id=0, has_side_effects=True),
-    )(waves, potential.reshape(1, CUBE**3), atom_points, projectors, coupling)
+        compiler_params=pltpu.CompilerParams(collective_id=0, has_side_effects=True, vmem_limit_bytes=12 << 20),
+    )(
+        *(
+            pltpu.with_memory_space_constraint(value, pltpu.MemorySpace.HBM)
+            for value in (waves, potential.reshape(1, CUBE**3), atom_points, projectors, coupling)
+        )
+    )
 
 
 def solution(mesh):

time: 65.3 us -> 63.1 us (0.966)
  Pallas kernels: 63.3 us -> 62.2 us
  local copies, waits for them, and re-layouts: 1.67 us -> 0.71 us
    pallas_call x1, Pallas kernels: 63.3 us -> 62.2 us  [local(): pl.pallas_call(kernel, out_shape=jax.ShapeDtypeStruct((BAND_LOC, CUBE **...]
    unnamed x1, local copies, waits for them, and re-layouts: 1.67 us -> 0.71 us
where the time goes in v4:
time: 63.1 us; the launch traced here: 62.9 us
  Pallas kernels  62.2 us (99%)
  local copies, waits for them, and re-layouts  0.71 us (1%)
    pallas_call x1, Pallas kernels, local(): pl.pallas_call(kernel, out_shape=jax.ShapeDtypeStruct((BAND_LOC, CUBE **...  62.2 us

profile of v4, /device:TPU:1, one launch (start us, length us, event | category | flops | bytes accessed | tf_op | source)
XLA Modules:
  0.0 62.9 jit_solution(4747550792195068414)
XLA Ops:
  0.0 62.2 %shard_map.55 = f32[16,4096]{1,0:T(8,128)S(1)} custom-call(f32[16,4096]{1,0:T(8,128)} %waves.1, f32[1,4096]{1,0:T(1,128)} %bitcast.1, s32[4,256]{1,0:T(4,128)} %pts.1, f32[4,8,256]{2,1,0:T(8,128)} %proj.1, f32[4,8,8]{2,1,0:T(8,128)} %coup.1), custom_call_target="tpu_custom_call" | custom-call | tf_op jit(solution)/shard_map/pallas_call | solution.py:467
  62.2 0.7 %copy.7 = f32[16,4096]{1,0:T(8,128)} copy(f32[16,4096]{1,0:T(8,128)S(1)} %shard_map.55) | data formatting | bytes 524288

commit v5 on v4

--- a/solution.py
+++ b/solution.py
@@ -167,23 +167,32 @@
         inner = dot(vh, stencil[0:256, :]) + dot(vl, stencil[0:256, :])
         return pterm[...] * here + added + (1.0 / 96.0) * inner
 
-    def outside(turn, ref):
-        for face in halo(turn, ref):
-            under(face[1], face[2].wait_recv)
+    def from_faces(turn, slots):
         wide = jnp.concatenate(
             [
                 jnp.concatenate(
                     [jnp.where(group == g, facerecv[turn, slot], 0.0) for g in range(4)], axis=0
                 )
-                for slot in range(3)
+                for slot in slots
             ],
             axis=1,
         )
         wh, wl = split(wide)
-        outer = dot(wh, stencil[256:640, :]) + dot(wl, stencil[256:640, :])
+        table = stencil[256 + 128 * slots[0] : 384 + 128 * slots[-1], :]
+        return jnp.concatenate(
+            [dot(wh[r : r + 128], table) + dot(wl[r : r + 128], table) for r in (0, 128)], axis=0
+        )
+
+    def outside(turn, ref):
+        faces = halo(turn, ref)
+        for slot in (2, 3, 4):
+            under(faces[slot][1], faces[slot][2].wait_recv)
         far = ref[0:256, :] + ref[64:320, :]
         near = ref[16:272, :] + ref[48:304, :]
-        return (1.0 / 96.0) * (outer + (far - 16.0 * near))
+        value = from_faces(turn, (2,)) + (far - 16.0 * near)
+        for slot in (0, 1):
+            under(faces[slot][1], faces[slot][2].wait_recv)
+        return (1.0 / 96.0) * (value + from_faces(turn, (0, 1)))
 
     row, col = iota((PLANE, 128), 0), iota((PLANE, 128), 1)
     ry, rz = row >> 4, row & 15
@@ -267,27 +276,38 @@
             device_id=(dom, peer), device_id_type=MESH,
         )
 
+    def each(count, me, action):
+        for k in range(count - 1):
+            step = count // 2 + (1 - 2 * (k % 2)) * ((k + 1) // 2)
+            action(lax.rem(me + step, count))
+
     def peers(count, me, action):
         @pl.loop(0, count - 1)
         def _(k):
             step = count // 2 + (1 - 2 * lax.rem(k, 2)) * ((k + 1) // 2)
             action(lax.rem(me + step, count))
 
-    peers(NBAND, band, lambda peer: to_piece(peer).start())
+    each(NBAND, band, lambda peer: to_piece(peer).start())
     mine = pl.ds(pl.multiple_of(band * 16, 16), 16)
     work[mine, PLANE : 2 * PLANE] = fs[mine, :]
-    peers(NBAND, band, lambda peer: from_piece(peer).wait_recv())
+    each(NBAND, band, lambda peer: from_piece(peer).wait_recv())
 
     piece = work[:, PLANE : 2 * PLANE]
     ph, plo = split(piece)
-    gram = (1.0 / POINTS) * (dot(ph, ph, 1, 1) + (dot(ph, plo, 1, 1) + dot(plo, ph, 1, 1)))
+    def product(i, n):
+        h, l = ph[i : i + 128], plo[i : i + 128]
+        return (1.0 / POINTS) * (
+            dot(h, ph[0:n], 1, 1) + (dot(h, plo[0:n], 1, 1) + dot(l, ph[0:n], 1, 1))
+        )
+
+    upper, lower = product(0, 128), product(128, 256)
     row, col = iota((128, 128), 0), iota((128, 128), 1)
-    low = gram[128:256, 128:256]
-    packed = jnp.where(row >= col, gram[0:128, 0:128], low)
+    low = lower[:, 128:256]
+    packed = jnp.where(row >= col, upper, low)
     diag = jnp.sum(jnp.where(row == col, low, 0.0), axis=0, keepdims=True)
     for c in range(NSET):
         part[c, 0:16, :] = packed[16 * c : 16 * c + 16, :]
-        part[c, 16:32, :] = gram[128 + 16 * c : 144 + 16 * c, 0:128]
+        part[c, 16:32, :] = lower[16 * c : 16 * c + 16, 0:128]
         part[c, 32:33, :] = diag
 
     def chunk(src, dst, send, recv, where):
@@ -296,11 +316,11 @@
         )
 
     def share(count, me, at, buf, send, recv):
-        peers(count, me, lambda peer: chunk(
+        each(count, me, lambda peer: chunk(
             buf.at[me], buf.at[me], send.at[peer], recv.at[me], at(peer)).start())
 
     def collect(count, me, at, buf, send, recv):
-        peers(count, me, lambda peer: chunk(
+        each(count, me, lambda peer: chunk(
             buf.at[me], buf.at[peer], send.at[peer], recv.at[peer], at(peer)).wait_recv())
 
     def drain(count, me, at, buf, send, recv):
@@ -313,10 +333,10 @@
             value = value + buf[i]
         return value
 
-    peers(NSET, mine_set, lambda peer: chunk(
+    each(NSET, mine_set, lambda peer: chunk(
         part.at[peer], rs_buf.at[mine_set], r_send.at[peer], r_recv.at[mine_set], at_set(peer)).start())
     rs_buf[mine_set] = part[mine_set]
-    peers(NSET, mine_set, lambda peer: chunk(
+    each(NSET, mine_set, lambda peer: chunk(
         part.at[peer], rs_buf.at[peer], r_send.at[peer], r_recv.at[peer], at_set(peer)).wait_recv())
     value = total(rs_buf, NSET)
     a_y = (NY, py, at_y, ay_buf, s_send.at[0], s_recv.at[0])
@@ -350,19 +370,19 @@
     work[128:256, 0:128] = cross
     work[0:128, 128:256] = cross.T
 
-    def to_out(peer):
+    def to_out(peer, half):
         return pltpu.make_async_remote_copy(
-            src_ref=fs.at[pl.ds(pl.multiple_of(peer * 16, 16), 16), :],
-            dst_ref=out.at[:, pl.ds(pl.multiple_of(band * PLANE, PLANE), PLANE)],
-            send_sem=o_send.at[peer], recv_sem=o_recv.at[band],
+            src_ref=fs.at[pl.ds(pl.multiple_of(peer * 16 + 8 * half, 8), 8), :],
+            dst_ref=out.at[pl.ds(8 * half, 8), pl.ds(pl.multiple_of(band * PLANE, PLANE), PLANE)],
+            send_sem=o_send.at[half, peer], recv_sem=o_recv.at[half, band],
             device_id=(dom, peer), device_id_type=MESH,
         )
 
-    def from_out(peer):
+    def from_out(peer, half):
         return pltpu.make_async_remote_copy(
-            src_ref=fs.at[pl.ds(0, 16), :],
-            dst_ref=out.at[:, pl.ds(pl.multiple_of(peer * PLANE, PLANE), PLANE)],
-            send_sem=o_send.at[peer], recv_sem=o_recv.at[peer],
+            src_ref=fs.at[pl.ds(0, 8), :],
+            dst_ref=out.at[pl.ds(8 * half, 8), pl.ds(pl.multiple_of(peer * PLANE, PLANE), PLANE)],
+            send_sem=o_send.at[half, peer], recv_sem=o_recv.at[half, peer],
             device_id=(dom, peer), device_id_type=MESH,
         )
 
@@ -423,15 +443,11 @@
                 cols = coming
             scale = lax.rsqrt(pivots)
             tiles[s] = [v * scale for v in tiles[s]]
+            fs[first + 8 * s : first + 8 * s + 8, 0:128] = tiles[s][-2]
+            fs[first + 8 * s : first + 8 * s + 8, 128:256] = tiles[s][-1]
+            peer = j * (BLOCK // 16) + s // 2
+            pl.when(peer != band)(to_out(peer, s % 2).start)
         lanes = [jnp.concatenate([tiles[t][c] for t in range(count)], axis=0) for c in range((512 - lo) // 128)]
-        fs[first : first + BLOCK, 0:128] = lanes[-2]
-        fs[first : first + BLOCK, 128:256] = lanes[-1]
-        for half in range(BLOCK // 16):
-            peer = j * (BLOCK // 16) + half
-
-            @pl.when(peer != band)
-            def _():
-                to_out(peer).start()
 
         after = first + BLOCK
         if after < 256:
@@ -456,8 +472,10 @@
         part.at[peer], rs_buf.at[peer], r_send.at[peer], r_recv.at[peer], at_set(peer)).wait_send())
     for stage in (a_y, b_z, a_z, b_y, a_set):
         drain(*stage)
-    peers(NBAND, band, lambda peer: from_out(peer).wait_recv())
-    peers(NBAND, band, lambda peer: to_out(peer).wait_send())
+    for half in range(2):
+        peers(NBAND, band, lambda peer: from_out(peer, half).wait_recv())
+    for half in range(2):
+        peers(NBAND, band, lambda peer: to_out(peer, half).wait_send())
     own.wait()
 
 
@@ -480,7 +498,7 @@
             vmem((NY, 16, 128), F32), vmem((NZ, 16, 128), F32),
             vmem((NZ, 17, 128), F32), vmem((NY, 17, 128), F32), vmem((NSET, ROWS, 128), F32),
             dma((20,)), dma((2, 5)), dma((2, 5)), dma((16,)), dma((16,)), dma((8,)), dma((8,)),
-            dma((5, 8)), dma((5, 8)), dma((16,)), dma((16,)), dma,
+            dma((5, 8)), dma((5, 8)), dma((2, 16)), dma((2, 16)), dma,
         ],
         compiler_params=pltpu.CompilerParams(collective_id=0, has_side_effects=True, vmem_limit_bytes=12 << 20),
     )(

time: 63.1 us -> 62.9 us (level)
  no operation moved by 1% of the time
where the time goes in v5:
time: 62.9 us; the launch traced here: 62.4 us
  Pallas kernels  61.7 us (98%)
  local copies, waits for them, and re-layouts  0.71 us (1%)
    pallas_call x1, Pallas kernels, local(): pl.pallas_call(kernel, out_shape=jax.ShapeDtypeStruct((BAND_LOC, CUBE **...  61.7 us

profile of v5, /device:TPU:1, one launch (start us, length us, event | category | flops | bytes accessed | tf_op | source)
XLA Modules:
  0.0 62.4 jit_solution(11772850087966573424)
XLA Ops:
  0.0 61.7 %shard_map.55 = f32[16,4096]{1,0:T(8,128)S(1)} custom-call(f32[16,4096]{1,0:T(8,128)} %waves.1, f32[1,4096]{1,0:T(1,128)} %bitcast.1, s32[4,256]{1,0:T(4,128)} %pts.1, f32[4,8,256]{2,1,0:T(8,128)} %proj.1, f32[4,8,8]{2,1,0:T(8,128)} %coup.1), custom_call_target="tpu_custom_call" | custom-call | tf_op jit(solution)/shard_map/pallas_call | solution.py:485
  61.7 0.7 %copy.7 = f32[16,4096]{1,0:T(8,128)} copy(f32[16,4096]{1,0:T(8,128)S(1)} %shard_map.55) | data formatting | bytes 524288

commit v6 on v5

--- a/solution.py
+++ b/solution.py
@@ -454,12 +454,9 @@
             base = after // 128 * 128
             rest = jnp.concatenate(lanes[(base - lo) // 128 :], axis=1)
             high, low = split(rest)
-            lead = high[:, 0 : 256 - base].astype(F32)
-            left = jnp.concatenate([lead, lead, rest[:, 0 : 256 - base] - lead], axis=0).T
-            left = left[after - base :, :].astype(BF16)
-            work[after:256, base:512] = work[after:256, base:512] - dot(
-                left, jnp.concatenate([high, low, high], axis=0)
-            )
+            left = jnp.concatenate([high, high, low], axis=0)[:, 0 : 256 - base]
+            update = dot(left, jnp.concatenate([high, low, high], axis=0), 0, 0)
+            work[after:256, base:512] = work[after:256, base:512] - update[after - base :]
 
     own = pltpu.make_async_copy(
         fs.at[mine, :], out.at[:, pl.ds(pl.multiple_of(band * PLANE, PLANE), PLANE)], o_own
@@ -472,11 +469,11 @@
         part.at[peer], rs_buf.at[peer], r_send.at[peer], r_recv.at[peer], at_set(peer)).wait_send())
     for stage in (a_y, b_z, a_z, b_y, a_set):
         drain(*stage)
-    for half in range(2):
-        peers(NBAND, band, lambda peer: from_out(peer, half).wait_recv())
+    own.wait()
     for half in range(2):
         peers(NBAND, band, lambda peer: to_out(peer, half).wait_send())
-    own.wait()
+    for half in range(2):
+        each(NBAND, band, lambda peer: from_out(peer, half).wait_recv())
 
 
 def local(waves, potential, atom_points, projectors, coupling):

time: 62.9 us -> 62.6 us (level)
  no operation moved by 1% of the time
where the time goes in v6:
time: 62.6 us; the launch traced here: 62.4 us
  Pallas kernels  61.7 us (99%)
  local copies, waits for them, and re-layouts  0.71 us (1%)
    pallas_call x1, Pallas kernels, local(): pl.pallas_call(kernel, out_shape=jax.ShapeDtypeStruct((BAND_LOC, CUBE **...  61.7 us

profile of v6, /device:TPU:1, one launch (start us, length us, event | category | flops | bytes accessed | tf_op | source)
XLA Modules:
  0.0 62.4 jit_solution(641403795657356301)
XLA Ops:
  0.0 61.7 %shard_map.55 = f32[16,4096]{1,0:T(8,128)S(1)} custom-call(f32[16,4096]{1,0:T(8,128)} %waves.1, f32[1,4096]{1,0:T(1,128)} %bitcast.1, s32[4,256]{1,0:T(4,128)} %pts.1, f32[4,8,256]{2,1,0:T(8,128)} %proj.1, f32[4,8,8]{2,1,0:T(8,128)} %coup.1), custom_call_target="tpu_custom_call" | custom-call | tf_op jit(solution)/shard_map/pallas_call | solution.py:482
  61.7 0.7 %copy.7 = f32[16,4096]{1,0:T(8,128)} copy(f32[16,4096]{1,0:T(8,128)S(1)} %shard_map.55) | data formatting | bytes 524288
